TPU v7x, 32 devices: a whole 2x2x4 slice. The times are simulated.
32 devices in a mesh: row: 8 (over z, y), col: 4 (over x, core).
Axes of the slice: x: 2, y: 2, z: 4, core: 2. Of those that a mesh axis runs over, the one named last changes fastest.
Arguments:
- matrix: float32 [6144, 16384], P('row', 'col'), may hold values from -6 to 6
Outputs:
- updated: float32 [6144, 16384], P('row', 'col')
All inputs are finite; a program needn't handle non-finite values.
Results may differ from a plain program's by a relative error of at most 0.0003.
Values sent between devices are 32-bit elements; how exact they have to be, the bound alone decides.
A program may use at most 128 MiB of HBM per device.

v0:
```python
import functools

import jax
import jax.numpy as jnp
from jax import lax
from jax.experimental import pallas as pl
from jax.experimental.pallas import tpu as pltpu
from jax.sharding import PartitionSpec as P

PANEL = 128
STRIP = 8
LANES = 128
MESH = pl.DeviceIdType.MESH


def dot_exact(a, b, contract):
    return lax.dot_general(
        a, b, (contract, ((), ())), precision=lax.Precision.HIGHEST, preferred_element_type=jnp.float32
    )


def factor_values(gram, top, between=lambda strip: None):
    strips = PANEL // STRIP
    rows = lax.broadcasted_iota(jnp.int32, (STRIP, 1), 0)
    eye = (
        lax.broadcasted_iota(jnp.int32, (PANEL, PANEL), 0) == lax.broadcasted_iota(jnp.int32, (PANEL, PANEL), 1)
    ).astype(jnp.float32)
    chol = jnp.concatenate([gram, eye], axis=1)
    work = jnp.concatenate([top, jnp.zeros_like(top)], axis=1)
    factor_rows = []
    lanes = lax.broadcasted_iota(jnp.int32, (STRIP, 2 * PANEL), 1)
    previous = None
    for strip in range(strips + 1):
        at, back = strip * STRIP, (strip - 1) * STRIP
        if strip < strips:
            between(strip)
            panel = chol[:STRIP]
            scale = jnp.ones((STRIP, 1), jnp.float32)
        if strip > 0:
            inner = work[back : back + STRIP] + previous
            aside = work[:, back : back + STRIP]
        for j in range(STRIP):
            if strip < strips:
                column = panel[:, at + j : at + j + 1]
                pivot = column[j : j + 1]
                multiplier = jnp.where(rows > j, column / pivot, 0.0)
            if strip > 0:
                inner_column = inner[:, back + j : back + j + 1]
                pivot_row = inner[j : j + 1] / inner_column[j : j + 1]
            if strip < strips:
                scale = jnp.where(rows == j, lax.rsqrt(pivot), scale)
                panel = panel - multiplier * panel[j : j + 1]
            if strip > 0:
                inner = jnp.where(rows == j, pivot_row, inner - inner_column * pivot_row)
        if strip < strips:
            panel = jnp.where(lanes >= at + rows, panel * scale, 0.0)
            factor_rows.append(panel[:, :PANEL])
            if strip < strips - 1:
                chol = chol[STRIP:] - dot_exact(panel[:, at + STRIP : PANEL], panel, ((0,), (0,)))
        if strip > 0:
            update = dot_exact(aside, inner, ((1,), (0,)))
            pieces = []
            if back > 0:
                pieces.append(work[:back] - update[:back])
            pieces.append(inner)
            if strip < strips:
                pieces.append(work[at:] - update[at:])
            work = jnp.concatenate(pieces, axis=0)
        previous = panel
    return jnp.concatenate(factor_rows, axis=0), work[:, PANEL:]


def everyone_ready(n_row, n_col):
    row, col = lax.axis_index("row"), lax.axis_index("col")
    barrier = pltpu.get_barrier_semaphore()
    for d in range(1, n_row):
        pl.semaphore_signal(barrier, inc=1, device_id={"row": lax.rem(row + d, n_row)}, device_id_type=MESH)
    for d in range(1, n_col):
        pl.semaphore_signal(barrier, inc=1, device_id={"col": lax.rem(col + d, n_col)}, device_id_type=MESH)
    pl.semaphore_wait(barrier, n_row - 1 + max(n_col - 1, 0))


def send(src, dst, send_sem, recv_sem, target):
    return pltpu.make_async_remote_copy(
        src_ref=src, dst_ref=dst, send_sem=send_sem, recv_sem=recv_sem, device_id=target, device_id_type=MESH
    )


def split(x):
    high = x.astype(jnp.bfloat16)
    return high, (x - high.astype(jnp.float32)).astype(jnp.bfloat16)


def step_kernel(
    n_row, n_col, inner_n, chunks, matrix_ref, shifted_out, hold,
    block, partial, stacked, pair_in, half, far_in, top_in, panel, top, parts, arrived, whole,
    local_sem, block_sem, own_sem,
    panel_send, top_send, part_send, whole_send, share_send, scatter_send,
    panel_recv, top_recv, part_recv, whole_recv, share_recv, scatter_recv,
    pair_send, far_send, done_send, back_send, pair_recv, far_recv, done_recv, back_recv,
):
    row, col = lax.axis_index("row"), lax.axis_index("col")
    piece = PANEL // n_row
    outer_n = n_row // inner_n
    outer, inner = row // inner_n, lax.rem(row, inner_n)
    other = 1 - inner
    partner = {"row": outer * inner_n + other}
    span = outer_n * LANES
    everyone_ready(n_row, n_col)

    def load(k):
        place = pl.ds(k * inner_n * span, inner_n * span)
        return pltpu.make_async_copy(matrix_ref.at[:, place], block.at[:, place], block_sem.at[k])

    def scatter(k, r):
        place = pl.ds((k * inner_n + r % inner_n) * span + r // inner_n * LANES, LANES)
        return send(
            matrix_ref.at[pl.ds(0, PANEL), place], top_in.at[k],
            scatter_send.at[k, r - 1], scatter_recv.at[k], {"row": r},
        )

    def keep(k):
        place = pl.ds(k * inner_n * span, LANES)
        return pltpu.make_async_copy(matrix_ref.at[pl.ds(0, PANEL), place], top_in.at[k], own_sem.at[k])

    def start_scatter():
        for k in range(chunks):
            for r in range(1, n_row):
                scatter(k, r).start()
            keep(k).start()

    def columns(k, i):
        return pl.ds(pl.multiple_of((k * inner_n + i) * span, span), span)

    def peer(d):
        return lax.rem(outer + d, outer_n)

    def pair(k):
        return send(partial.at[:, columns(k, other)], pair_in.at[k], pair_send.at[k], pair_recv.at[k], partner)

    def far(k, d):
        q = peer(d)
        return send(
            half.at[k, q], far_in.at[k, d - 1], far_send.at[k, d - 1], far_recv.at[k, d - 1],
            {"row": q * inner_n + inner},
        )

    def spot(k, o):
        return pl.ds(pl.multiple_of((k * inner_n + inner) * span + o * LANES, LANES), LANES)

    def done(k, d):
        return send(
            hold.at[:, spot(k, outer)], hold.at[:, spot(k, outer)], done_send.at[k, d - 1], done_recv.at[k, d - 1],
            {"row": peer(d) * inner_n + inner},
        )

    def back(k):
        return send(hold.at[:, columns(k, inner)], hold.at[:, columns(k, inner)], back_send.at[k], back_recv.at[k], partner)

    def multiply(k, i):
        place = columns(k, i)
        high, low = split(block[:, place])
        both = jnp.dot(stacked[...], high, preferred_element_type=jnp.float32)
        rest = jnp.dot(stacked[:PANEL], low, preferred_element_type=jnp.float32)
        partial[:, place] = both[:PANEL] + both[PANEL:] + rest

    def prepare():
        for k in range(chunks):
            load(k).wait()
        high, low = split(jnp.transpose(panel[...]))
        stacked[:PANEL] = high
        stacked[PANEL:] = low

    @pl.when((row == 0) & (col != 0))
    def _():
        start_scatter()

    @pl.when(col == 0)
    def _():
        fetch = pltpu.make_async_copy(matrix_ref.at[:, pl.ds(0, PANEL)], panel, local_sem.at[0])
        fetch.start()
        fetch.wait()
        for k in range(chunks):
            load(k).start()
        panel_copies = [
            send(panel, panel, panel_send.at[c - 1], panel_recv.at[0], {"col": c}) for c in range(1, n_col)
        ]

        @pl.when(row == 0)
        def _():
            for r in range(1, n_row):
                send(panel.at[pl.ds(0, PANEL)], top, top_send.at[r - 1], top_recv.at[0], {"row": r}).start()
            own = pltpu.make_async_copy(panel.at[pl.ds(0, PANEL)], top, local_sem.at[1])
            own.start()
            own.wait()

        local = dot_exact(panel[...], panel[...], ((0,), (0,)))
        for q in range(n_row):
            parts[q] = local[q * piece : (q + 1) * piece]
        part_copies = []
        for d in range(1, n_row):
            q = lax.rem(row + d, n_row)
            part_copies.append(
                send(parts.at[q], arrived.at[d - 1], part_send.at[d - 1], part_recv.at[d - 1], {"row": q})
            )
            part_copies[-1].start()
        for copy in panel_copies:
            copy.start()
        prepare()
        early = min(2, chunks)
        for k in range(early):
            multiply(k, other)
        total = parts[row]
        for d in range(1, n_row):
            part_copies[d - 1].wait_recv()
            total = total + arrived[d - 1]
        whole[row] = total
        whole_copies = []
        for d in range(1, n_row):
            q = lax.rem(row + d, n_row)
            whole_copies.append(
                send(whole.at[row], whole.at[row], whole_send.at[d - 1], whole_recv.at[d - 1], {"row": q})
            )
            whole_copies[-1].start()
        for k in range(early, chunks):
            multiply(k, other)
        for k in range(chunks):
            pair(k).start()

        @pl.when(row == 0)
        def _():
            start_scatter()

        @pl.when(row != 0)
        def _():
            send(top, top, top_send.at[0], top_recv.at[0], {"row": 0}).wait_recv()

        for d in range(1, n_row):
            q = lax.rem(row - d + n_row, n_row)
            send(whole.at[q], whole.at[q], whole_send.at[d - 1], whole_recv.at[d - 1], {"row": q}).wait_recv()
        shares = []
        for c in range(1, n_col):
            shares.append(send(top, top, share_send.at[2 * c - 2], share_recv.at[0], {"col": c}))
            shares.append(send(whole, whole, share_send.at[2 * c - 1], share_recv.at[1], {"col": c}))
        for copy in shares:
            copy.start()

        @pl.when(row == 0)
        def _():
            for r in range(1, n_row):
                send(panel.at[pl.ds(0, PANEL)], top, top_send.at[r - 1], top_recv.at[0], {"row": r}).wait_send()

        for copy in part_copies + panel_copies + whole_copies + shares:
            copy.wait_send()

    @pl.when(col != 0)
    def _():
        for k in range(chunks):
            load(k).start()
        root = {"col": 0}
        send(panel, panel, panel_send.at[0], panel_recv.at[0], root).wait_recv()
        prepare()
        for k in range(chunks):
            multiply(k, other)
            pair(k).start()
        send(top, top, share_send.at[0], share_recv.at[0], root).wait_recv()
        send(whole, whole, share_send.at[1], share_recv.at[1], root).wait_recv()

    def stage_far(k):
        pair(k).wait_recv()
        for o in range(outer_n):
            half[k, o] = partial[:, spot(k, o)] + pair_in[k, :, o * LANES : (o + 1) * LANES]
        for d in range(1, outer_n):
            far(k, d).start()

    def stage_done(k, factor, inverse):
        total = half[k, outer]
        for d in range(1, outer_n):
            far(k, d).wait_recv()
            total = total + far_in[k, d - 1]

        @pl.when(row == 0)
        def _():
            keep(k).wait()

        @pl.when(row != 0)
        def _():
            send(top_in.at[k], top_in.at[k], scatter_send.at[k, 0], scatter_recv.at[k], {"row": 0}).wait_recv()

        total = total + dot_exact(factor, top_in[k], ((0,), (0,)))
        hold[:, spot(k, outer)] = dot_exact(inverse, total, ((1,), (0,)))
        for d in range(1, outer_n):
            done(k, d).start()

    def stage_back(k):
        for d in range(1, outer_n):
            q = lax.rem(outer - d + outer_n, outer_n)
            send(
                hold.at[:, spot(k, q)], hold.at[:, spot(k, q)], done_send.at[k, d - 1], done_recv.at[k, d - 1],
                {"row": q * inner_n + inner},
            ).wait_recv()
        back(k).start()

    gram = jnp.concatenate([whole[q] for q in range(n_row)], axis=0)

    def between(strip):
        if strip < chunks:
            multiply(strip, inner)
        elif strip >= first_far and (strip - first_far) % 3 == 0 and (strip - first_far) // 3 < ready:
            stage_far((strip - first_far) // 3)

    first_far = 2 * chunks
    ready = max(0, min(chunks - 1, (PANEL // STRIP - first_far + 2) // 3))
    factor, inverse = factor_values(gram, top[...], between)
    for step in range(chunks + 2):
        if step < ready:
            stage_done(step, factor, inverse)
        if ready + step < chunks:
            stage_far(ready + step)
        if ready <= step < chunks:
            stage_done(step, factor, inverse)
        if 0 <= step - 2 < chunks:
            stage_back(step - 2)
    shifted_out[...] = panel[...]

    @pl.when(row == 0)
    def _():
        shifted_out[:PANEL] = panel[:PANEL] + factor
        for k in range(chunks):
            for r in range(1, n_row):
                scatter(k, r).wait_send()

    for k in range(chunks):
        mirror = hold.at[:, columns(k, other)]
        send(mirror, mirror, back_send.at[k], back_recv.at[k], partner).wait_recv()
    for k in range(chunks):
        pair(k).wait_send()
        back(k).wait_send()
        for d in range(1, outer_n):
            far(k, d).wait_send()
            done(k, d).wait_send()


def whole_step(matrix, n_row, n_col):
    height, width = matrix.shape
    piece = PANEL // n_row
    inner_n = 2
    outer_n = n_row // inner_n
    chunks = width // (n_row * LANES)
    span = outer_n * LANES
    dma = pltpu.SemaphoreType.DMA
    f32 = jnp.float32
    return pl.pallas_call(
        functools.partial(step_kernel, n_row, n_col, inner_n, chunks),
        out_shape=(jax.ShapeDtypeStruct((height, PANEL), f32), jax.ShapeDtypeStruct((PANEL, width), f32)),
        in_specs=[pl.BlockSpec(memory_space=pl.ANY)],
        out_specs=(pl.BlockSpec(memory_space=pltpu.VMEM),) * 2,
        scratch_shapes=[
            pltpu.VMEM((height, width), f32),
            pltpu.VMEM((PANEL, width), f32),
            pltpu.VMEM((2 * PANEL, height), jnp.bfloat16),
            pltpu.VMEM((chunks, PANEL, span), f32),
            pltpu.VMEM((chunks, outer_n, PANEL, LANES), f32),
            pltpu.VMEM((chunks, outer_n - 1, PANEL, LANES), f32),
            pltpu.VMEM((chunks, PANEL, LANES), f32),
            pltpu.VMEM((height, PANEL), f32),
            pltpu.VMEM((PANEL, PANEL), f32),
            pltpu.VMEM((n_row, piece, PANEL), f32),
            pltpu.VMEM((n_row - 1, piece, PANEL), f32),
            pltpu.VMEM((n_row, piece, PANEL), f32),
            dma((2,)),
            dma((chunks,)),
            dma((chunks,)),
            dma((n_col - 1,)),
            dma((n_row - 1,)),
            dma((n_row - 1,)),
            dma((n_row - 1,)),
            dma((2 * n_col - 2,)),
            dma((chunks, n_row - 1)),
            dma((1,)),
            dma((1,)),
            dma((n_row - 1,)),
            dma((n_row - 1,)),
            dma((2,)),
            dma((chunks,)),
            dma((chunks,)),
            dma((chunks, outer_n - 1)),
            dma((chunks, outer_n - 1)),
            dma((chunks,)),
            dma((chunks,)),
            dma((chunks, outer_n - 1)),
            dma((chunks, outer_n - 1)),
            dma((chunks,)),
        ],
        compiler_params=pltpu.CompilerParams(
            collective_id=0, has_side_effects=True, vmem_limit_bytes=48 * 1024 * 1024
        ),
        name="whole_step",
    )(matrix)


def on_device(n_row, n_col, matrix):
    shifted, coefficients = whole_step(matrix, n_row, n_col)
    return matrix - jnp.dot(shifted, coefficients, precision=lax.Precision.HIGH)


def solution(mesh):
    body = functools.partial(on_device, mesh.shape["row"], mesh.shape["col"])
    return jax.shard_map(body, mesh=mesh, in_specs=(P("row", "col"),), out_specs=P("row", "col"), check_vma=False)
```

profile of v0, /device:TPU:28, one launch (start us, length us, event | category | flops | bytes accessed | tf_op | source)
XLA Modules:
  0.0 108.0 jit_solution(14633575635359978024)
XLA Ops:
  0.0 0.0 copy-start
  0.0 100.0 %whole_step.1 = (f32[768,128]{1,0:T(8,128)S(1)}, f32[128,4096]{1,0:T(8,128)S(1)}) custom-call(f32[768,4096]{1,0:T(8,128)} %matrix_ref.1), custom_call_target="tpu_custom_call" | custom-call | tf_op jit(solution)/shard_map/whole_step/pallas_call | solution.py:353
  100.0 0.0 copy-done
  100.0 8.0 %convolution_subtract_fusion = f32[768,4096]{1,0:T(8,128)} fusion(f32[768,4096]{1,0:T(8,128)S(1)} %copy-done, f32[768,128]{1,0:T(8,128)S(1)} %get-tuple-element.7, f32[128,4096]{1,0:T(8,128)S(1)} %get-tuple-element.8), kind=kOutput, calls=%fused_computation | convolution fusion | flops 2419064832 | bytes 27656192 | tf_op jit(solution)/shard_map/dot_general | solution.py:404
Async XLA Ops:
  0.0 100.0 %copy-start = (f32[768,4096]{1,0:T(8,128)S(1)}, f32[768,4096]{1,0:T(8,128)}, u32[]{:S(2)}) copy-start(f32[768,4096]{1,0:T(8,128)} %matrix_ref.1) | copy-start | bytes 37748740
where the time goes:
time: 108 us
  Pallas kernels  100 us (93%)
  matrix products  7.96 us (7%)
    pallas_call x1, Pallas kernels, whole_step(): pl.pallas_call(functools.partial(step_kernel, n_row, n_col, inner_n, chun...  100 us
    dot_general x1, matrix products, on_device(): return matrix - jnp.dot(shifted, coefficients, precision=lax.Precision.HIGH)  7.96 us

commit v1 on v0

v1 whole, which is shorter than its diff:
```python
import functools

import jax
import jax.numpy as jnp
from jax import lax
from jax.experimental import pallas as pl
from jax.experimental.pallas import tpu as pltpu
from jax.sharding import PartitionSpec as P

PANEL = 128
STRIP = 8
LANES = 128
MESH = pl.DeviceIdType.MESH
EARLY = 4
MIX = 2
END_LAG = 3


def dot_exact(a, b, contract):
    return lax.dot_general(
        a, b, (contract, ((), ())), precision=lax.Precision.HIGHEST, preferred_element_type=jnp.float32
    )


def factor_values(gram, top, between=lambda strip: None):
    strips = PANEL // STRIP
    rows = lax.broadcasted_iota(jnp.int32, (STRIP, 1), 0)
    eye = (
        lax.broadcasted_iota(jnp.int32, (PANEL, PANEL), 0) == lax.broadcasted_iota(jnp.int32, (PANEL, PANEL), 1)
    ).astype(jnp.float32)
    chol = jnp.concatenate([gram, eye], axis=1)
    work = jnp.concatenate([top, jnp.zeros_like(top)], axis=1)
    factor_rows = []
    lanes = lax.broadcasted_iota(jnp.int32, (STRIP, 2 * PANEL), 1)
    previous = None
    for strip in range(strips + 1):
        at, back = strip * STRIP, (strip - 1) * STRIP
        if strip < strips:
            between(strip)
            panel = chol[:STRIP]
            scale = jnp.ones((STRIP, 1), jnp.float32)
        if strip > 0:
            inner = work[back : back + STRIP] + previous
            aside = work[:, back : back + STRIP]
        for j in range(STRIP):
            if strip < strips:
                column = panel[:, at + j : at + j + 1]
                pivot = column[j : j + 1]
                multiplier = jnp.where(rows > j, column / pivot, 0.0)
            if strip > 0:
                inner_column = inner[:, back + j : back + j + 1]
                pivot_row = inner[j : j + 1] / inner_column[j : j + 1]
            if strip < strips:
                scale = jnp.where(rows == j, lax.rsqrt(pivot), scale)
                panel = panel - multiplier * panel[j : j + 1]
            if strip > 0:
                inner = jnp.where(rows == j, pivot_row, inner - inner_column * pivot_row)
        if strip < strips:
            panel = jnp.where(lanes >= at + rows, panel * scale, 0.0)
            factor_rows.append(panel[:, :PANEL])
            if strip < strips - 1:
                chol = chol[STRIP:] - dot_exact(panel[:, at + STRIP : PANEL], panel, ((0,), (0,)))
        if strip > 0:
            update = dot_exact(aside, inner, ((1,), (0,)))
            pieces = []
            if back > 0:
                pieces.append(work[:back] - update[:back])
            pieces.append(inner)
            if strip < strips:
                pieces.append(work[at:] - update[at:])
            work = jnp.concatenate(pieces, axis=0)
        previous = panel
    return jnp.concatenate(factor_rows, axis=0), work[:, PANEL:]


def send(src, dst, send_sem, recv_sem, target):
    return pltpu.make_async_remote_copy(
        src_ref=src, dst_ref=dst, send_sem=send_sem, recv_sem=recv_sem, device_id=target, device_id_type=MESH
    )


def split(x):
    high = x.astype(jnp.bfloat16)
    return high, (x - high.astype(jnp.float32)).astype(jnp.bfloat16)


def step_kernel(
    n_row, n_col, matrix_ref, updated,
    partial, pair_in, chain_in, top_in, hold, stacked, shifted, panel, top, factor_ref, inverse_ref,
    parts, arrived, whole,
    fetch_sem, block_sem, own_sem,
    panel_send, panel_recv, part_send, part_recv, whole_send, whole_recv, top_send, top_recv, share_send, share_recv,
    scatter_send, scatter_recv, pair_send, pair_recv, chain_send, chain_recv,
    give_send, give_recv, pass_send, pass_recv,
):
    row, col = lax.axis_index("row"), lax.axis_index("col")
    width = updated.shape[1]
    blocks = width // (4 * LANES)
    piece = PANEL // n_row
    outer_n = n_row // 2
    last = outer_n - 1
    outer, inner = row // 2, lax.rem(row, 2)
    other = 1 - inner
    partner = {"row": outer * 2 + other}
    first, final = outer == 0, outer == last
    is_end = first | final
    mine = jnp.where(first, 0, 1)
    near = jnp.where(2 * outer < outer_n, 0, 1)
    far = 1 - near
    end_rows = [0, 1, n_row - 2, n_row - 1]

    barrier = pltpu.get_barrier_semaphore()
    for d in range(1, n_row):
        pl.semaphore_signal(barrier, inc=1, device_id={"row": lax.rem(row + d, n_row)}, device_id_type=MESH)
    for d in range(1, n_col):
        pl.semaphore_signal(barrier, inc=1, device_id={"col": lax.rem(col + d, n_col)}, device_id_type=MESH)

    def lanes(start, size):
        return pl.ds(pl.multiple_of(start, LANES), size)

    def unit(p, side):
        return lanes(p * (2 * LANES) + side * LANES, LANES)

    def load(j):
        place = lanes(j * (4 * LANES), 4 * LANES)
        return pltpu.make_async_copy(matrix_ref.at[:, place], updated.at[:, place], block_sem.at[j])

    def scatter(i, e):
        row_to = end_rows[e]
        place = unit(2 * i + e // 2, e % 2)
        return send(
            matrix_ref.at[pl.ds(0, PANEL), place], top_in.at[i], scatter_send.at[i, e], scatter_recv.at[i],
            {"row": row_to},
        )

    def keep(i):
        return pltpu.make_async_copy(matrix_ref.at[pl.ds(0, PANEL), unit(2 * i, 0)], top_in.at[i], own_sem.at[i])

    def start_scatter(i):
        @pl.when(row == 0)
        def _():
            for e in range(1, 4):
                scatter(i, e).start()

    def pair(p):
        return send(partial.at[:, unit(p, other)], pair_in.at[p], pair_send.at[p], pair_recv.at[p], partner)

    def chain(p, towards, own):
        slot = 0 if own else 1
        return send(
            partial.at[:, unit(p, inner if own else other)], chain_in.at[p, slot],
            chain_send.at[p, slot], chain_recv.at[p, slot], {"row": row + 2 * (2 * towards - 1)},
        )

    def is_direct(i, owner):
        return (owner == 1) & (lax.rem(i, MIX) != 0)

    def joins(owner):
        return outer == jnp.where(owner == 0, 1, last - 1)

    def owns(owner):
        return is_end & (owner == mine)

    def leads(owner):
        return is_end & (owner != mine)

    def give(p):
        place = unit(p, inner)
        return send(hold.at[:, place], hold.at[:, place], give_send.at[p], give_recv.at[p], partner)

    def given(p):
        place = unit(p, other)
        return send(hold.at[:, place], hold.at[:, place], give_send.at[p], give_recv.at[p], partner)

    def onward(p, owner, own):
        place = unit(p, inner if own else other)
        slot = 0 if own else 1
        return send(
            hold.at[:, place], hold.at[:, place], pass_send.at[p, slot], pass_recv.at[p, slot],
            {"row": row + 2 * (1 - 2 * owner)},
        )

    def multiply(j):
        place = lanes(j * (4 * LANES), 4 * LANES)
        high, low = split(updated[:, place])
        both = jnp.dot(stacked[...], high, preferred_element_type=jnp.float32)
        rest = jnp.dot(stacked[:PANEL], low, preferred_element_type=jnp.float32)
        partial[:, place] = both[:PANEL] + both[PANEL:] + rest

    def exchange(i):
        for side in range(2):
            p = 2 * i + side

            @pl.when(owns(side))
            def _():
                pair(p).start()

            @pl.when(leads(side))
            def _():
                chain(p, side, True).start()
                chain(p, side, False).start()

    def prepare():
        high, low = split(panel[...])
        shifted[:, :PANEL] = high
        shifted[:, PANEL:] = low
        high, low = split(jnp.transpose(panel[...]))
        stacked[:PANEL] = high
        stacked[PANEL:] = low

    def multiply_range(start, stop, ahead):
        @pl.loop(start, stop)
        def _(j):
            load(j).wait()
            multiply(j)
            exchange(j)

            @pl.when(j + ahead < blocks)
            def _():
                start_scatter(j + ahead)

    @pl.when(col == 0)
    def _():
        fetch = pltpu.make_async_copy(matrix_ref.at[:, pl.ds(0, PANEL)], panel, fetch_sem.at[0])
        fetch.start()
        fetch.wait()
        for j in range(blocks):
            load(j).start()
        local = dot_exact(panel[...], panel[...], ((0,), (0,)))
        for q in range(n_row):
            parts[q] = local[q * piece : (q + 1) * piece]

    @pl.when(col != 0)
    def _():
        for j in range(blocks):
            load(j).start()

    @pl.when(row == 0)
    def _():
        for i in range(blocks):
            keep(i).start()

    pl.semaphore_wait(barrier, n_row - 1 + n_col - 1)

    def panel_copy(to, slot):
        return send(panel, panel, panel_send.at[slot], panel_recv.at[0], {"col": to})

    heads = [1] + [c for c in range(2, n_col, 2)]

    @pl.when(col == 0)
    def _():
        def part(d):
            q = lax.rem(row + d, n_row)
            return send(parts.at[q], arrived.at[d - 1], part_send.at[d - 1], part_recv.at[d - 1], {"row": q})

        def whole_copy(e):
            return send(whole.at[row], whole.at[row], whole_send.at[e], whole_recv.at[row], {"row": end_rows[e]})

        def top_copy(e):
            return send(panel.at[pl.ds(0, PANEL)], top, top_send.at[e], top_recv.at[0], {"row": end_rows[e]})

        def share(c, slot):
            ref = (top, whole)[slot]
            return send(ref, ref, share_send.at[c - 1, slot], share_recv.at[slot], {"col": c})

        for d in range(1, n_row):
            part(d).start()
        for slot, c in enumerate(heads[1:]):
            panel_copy(c, slot + 1).start()

        @pl.when(row == 0)
        def _():
            for e in range(1, 4):
                top_copy(e).start()
            top[...] = panel[:PANEL]

        prepare()

        @pl.loop(0, blocks // 2)
        def _(j):
            load(j).wait()
            multiply(j)

        total = parts[row]
        for d in range(1, n_row):
            part(d).wait_recv()
            total = total + arrived[d - 1]
        whole[row] = total
        for e in range(4):
            @pl.when(row != end_rows[e])
            def _():
                whole_copy(e).start()

        panel_copy(heads[0], 0).start()

        @pl.loop(0, blocks // 2)
        def _(j):
            exchange(j)
            start_scatter(j)

        @pl.when(is_end)
        def _():
            @pl.when(row != 0)
            def _():
                send(top, top, top_send.at[0], top_recv.at[0], {"row": 0}).wait_recv()

            for c in range(1, n_col):
                share(c, 0).start()

        multiply_range(blocks // 2, blocks, 0)

        @pl.when(is_end)
        def _():
            for q in range(n_row):
                @pl.when(row != q)
                def _():
                    send(whole.at[q], whole.at[q], whole_send.at[0], whole_recv.at[q], {"row": q}).wait_recv()
            for c in range(1, n_col):
                share(c, 1).start()
            for c in range(1, n_col):
                share(c, 0).wait_send()
                share(c, 1).wait_send()

        for d in range(1, n_row):
            part(d).wait_send()
        for slot, c in enumerate(heads):
            panel_copy(c, slot).wait_send()
        for e in range(4):
            @pl.when(row != end_rows[e])
            def _():
                whole_copy(e).wait_send()

        @pl.when(row == 0)
        def _():
            for e in range(1, 4):
                top_copy(e).wait_send()

    @pl.when(col != 0)
    def _():
        for i in range(EARLY):
            @pl.when(col != 1)
            def _():
                start_scatter(i)
        root = {"col": 0}
        send(panel, panel, panel_send.at[0], panel_recv.at[0], root).wait_recv()
        relay = (lax.rem(col, 2) == 0) & (col + 1 < n_col)

        @pl.when(relay)
        def _():
            panel_copy(col + 1, 0).start()

        prepare()
        ahead = jnp.where(col == 1, 0, EARLY)
        multiply_range(0, blocks, ahead)

        @pl.when(is_end)
        def _():
            send(top, top, share_send.at[0, 0], share_recv.at[0], root).wait_recv()
            send(whole, whole, share_send.at[0, 1], share_recv.at[1], root).wait_recv()

        @pl.when(relay)
        def _():
            panel_copy(col + 1, 0).wait_send()

    def add(p, side, *terms):
        place = unit(p, side)
        total = partial[:, place]
        for term in terms:
            total = total + term[...]
        partial[:, place] = total

    def relay_sum(i, owner):
        p = 2 * i + owner
        chain(p, owner, True).wait_recv()
        add(p, inner, chain_in.at[p, 0])

        @pl.when(jnp.logical_not(joins(owner)))
        def _():
            chain(p, owner, True).start()

        chain(p, owner, False).wait_recv()
        add(p, other, chain_in.at[p, 1])

        @pl.when(joins(owner))
        def _():
            pair(p).start()

        @pl.when(jnp.logical_not(joins(owner)))
        def _():
            chain(p, owner, False).start()

    def join_sum(i, owner):
        @pl.when(joins(owner))
        def _():
            p = 2 * i + owner
            pair(p).wait_recv()
            add(p, inner, pair_in.at[p])
            chain(p, owner, True).start()

    @pl.when(is_end)
    def _():
        gram = jnp.concatenate([whole[q] for q in range(n_row)], axis=0)

        factor, inverse = factor_values(gram, top[...])
        factor_ref[...] = factor
        inverse_ref[:, :PANEL] = inverse
        inverse_ref[:, PANEL:] = dot_exact(inverse, factor, ((1,), (1,)))

        @pl.when(row == 0)
        def _():
            high, low = split(panel[:PANEL] + factor)
            shifted[:PANEL, :PANEL] = high
            shifted[:PANEL, PANEL:] = low

    @pl.when(jnp.logical_not(is_end))
    def _():
        @pl.loop(0, blocks + 2)
        def _(s):
            @pl.when(s >= 2)
            def _():
                join_sum(s - 2, near)

            @pl.when(s < blocks)
            def _():
                relay_sum(s, far)

            @pl.when((s >= 1) & (s <= blocks))
            def _():
                relay_sum(s - 1, near)

    def update(p):
        place = lanes(p * (2 * LANES), 2 * LANES)
        high, low = split(hold[:, place])
        both = jnp.dot(shifted[...], jnp.concatenate([high, high], axis=0), preferred_element_type=jnp.float32)
        rest = jnp.dot(shifted[:, :PANEL], low, preferred_element_type=jnp.float32)
        updated[:, place] = updated[:, place] - (both + rest)

    def solve(i):
        p = 2 * i + mine
        pair(p).wait_recv()
        chain(p, mine, True).wait_recv()

        @pl.when(row == 0)
        def _():
            keep(i).wait()

        @pl.when(row != 0)
        def _():
            send(top_in.at[i], top_in.at[i], scatter_send.at[i, 0], scatter_recv.at[i], {"row": 0}).wait_recv()

        place = unit(p, inner)
        total = partial[:, place] + pair_in[p] + chain_in[p, 0]
        hold[:, place] = dot_exact(inverse_ref[...], jnp.concatenate([total, top_in[i]], axis=0), ((1,), (0,)))
        onward(p, mine, True).start()
        give(p).start()

    def pass_other(i):
        p = 2 * i + mine

        @pl.when(is_direct(i, mine))
        def _():
            given(p).wait_recv()
            onward(p, mine, False).start()

    def accept(i, owner):
        p = 2 * i + owner
        stops = jnp.where(owner == 0, final, first)
        onward(p, owner, True).wait_recv()

        @pl.when(jnp.logical_not(stops))
        def _():
            onward(p, owner, True).start()

        @pl.when(is_direct(i, owner))
        def _():
            onward(p, owner, False).wait_recv()

            @pl.when(jnp.logical_not(stops))
            def _():
                onward(p, owner, False).start()

        @pl.when(jnp.logical_not(is_direct(i, owner)))
        def _():
            give(p).start()

    def finish(i, owner):
        p = 2 * i + owner

        @pl.when(jnp.logical_not(is_direct(i, owner)))
        def _():
            given(p).wait_recv()

        update(p)

    @pl.when(is_end)
    def _():
        @pl.loop(0, blocks + 2)
        def _(i):
            @pl.when(i < blocks)
            def _():
                solve(i)

            @pl.when(i >= 2)
            def _():
                pass_other(i - 2)

    def settle_sums(i, side):
        p = 2 * i + side

        @pl.when(owns(side) | joins(side))
        def _():
            pair(p).wait_send()

        @pl.when(jnp.logical_not(owns(side)))
        def _():
            chain(p, side, True).wait_send()

        @pl.when(jnp.logical_not(owns(side) | joins(side)))
        def _():
            chain(p, side, False).wait_send()

    def settle_back(i, side):
        p = 2 * i + side

        @pl.when(jnp.logical_not(leads(side)))
        def _():
            onward(p, side, True).wait_send()

            @pl.when(is_direct(i, side))
            def _():
                onward(p, side, False).wait_send()

        @pl.when(owns(side) | jnp.logical_not(is_direct(i, side)))
        def _():
            give(p).wait_send()

    wait = jnp.where(is_end, 0, 2)
    lag = jnp.where(is_end, END_LAG, 1)

    @pl.loop(0, blocks + END_LAG + 2)
    def _(s):
        @pl.when(s < blocks)
        def _():
            for side in range(2):
                settle_sums(s, side)

            @pl.when(row == 0)
            def _():
                for e in range(1, 4):
                    scatter(s, e).wait_send()

        @pl.when((s >= wait) & (s < blocks + wait))
        def _():
            finish(s - wait, near)

        @pl.when(jnp.logical_not(is_end) & (s < blocks))
        def _():
            accept(s, near)

        @pl.when((s >= lag + 2) & (s < blocks + lag + 2))
        def _():
            finish(s - lag - 2, far)

        @pl.when((s >= lag) & (s < blocks + lag))
        def _():
            accept(s - lag, far)

    @pl.loop(0, blocks)
    def _(i):
        for side in range(2):
            settle_back(i, side)


def flush_kernel(ready, out, sem):
    pieces = sem.shape[0]
    rows = out.shape[0] // pieces
    copies = [
        pltpu.make_async_copy(ready.at[pl.ds(q * rows, rows)], out.at[pl.ds(q * rows, rows)], sem.at[q])
        for q in range(pieces)
    ]
    for copy in copies:
        copy.start()
    for copy in copies:
        copy.wait()


def flush(ready):
    return pl.pallas_call(
        flush_kernel,
        out_shape=jax.ShapeDtypeStruct(ready.shape, ready.dtype),
        in_specs=[pl.BlockSpec(memory_space=pltpu.VMEM)],
        out_specs=pl.BlockSpec(memory_space=pl.ANY),
        scratch_shapes=[pltpu.SemaphoreType.DMA((8,))],
        compiler_params=pltpu.CompilerParams(vmem_limit_bytes=16 * 1024 * 1024),
        name="flush",
    )(ready)


def on_device(n_row, n_col, matrix):
    height, width = matrix.shape
    piece = PANEL // n_row
    blocks = width // (4 * LANES)
    pairs = 2 * blocks
    dma = pltpu.SemaphoreType.DMA
    f32, bf16 = jnp.float32, jnp.bfloat16
    ready = pl.pallas_call(
        functools.partial(step_kernel, n_row, n_col),
        out_shape=jax.ShapeDtypeStruct((height, width), f32),
        in_specs=[pl.BlockSpec(memory_space=pl.ANY)],
        out_specs=pl.BlockSpec(memory_space=pltpu.VMEM),
        scratch_shapes=[
            pltpu.VMEM((PANEL, width), f32),
            pltpu.VMEM((pairs, PANEL, LANES), f32),
            pltpu.VMEM((pairs, 2, PANEL, LANES), f32),
            pltpu.VMEM((blocks, PANEL, LANES), f32),
            pltpu.VMEM((PANEL, width), f32),
            pltpu.VMEM((2 * PANEL, height), bf16),
            pltpu.VMEM((height, 2 * PANEL), bf16),
            pltpu.VMEM((height, PANEL), f32),
            pltpu.VMEM((PANEL, PANEL), f32),
            pltpu.VMEM((PANEL, PANEL), f32),
            pltpu.VMEM((PANEL, 2 * PANEL), f32),
            pltpu.VMEM((n_row, piece, PANEL), f32),
            pltpu.VMEM((n_row - 1, piece, PANEL), f32),
            pltpu.VMEM((n_row, piece, PANEL), f32),
            dma((1,)),
            dma((blocks,)),
            dma((blocks,)),
            dma((n_col,)),
            dma((1,)),
            dma((n_row - 1,)),
            dma((n_row - 1,)),
            dma((4,)),
            dma((n_row,)),
            dma((4,)),
            dma((1,)),
            dma((n_col - 1, 2)),
            dma((2,)),
            dma((blocks, 4)),
            dma((blocks,)),
            dma((pairs,)),
            dma((pairs,)),
            dma((pairs, 2)),
            dma((pairs, 2)),
            dma((pairs,)),
            dma((pairs,)),
            dma((pairs, 2)),
            dma((pairs, 2)),
        ],
        compiler_params=pltpu.CompilerParams(
            collective_id=0, has_side_effects=True, vmem_limit_bytes=40 * 1024 * 1024
        ),
        name="whole_step",
    )(matrix)
    return flush(ready)


def solution(mesh):
    body = functools.partial(on_device, mesh.shape["row"], mesh.shape["col"])
    return jax.shard_map(body, mesh=mesh, in_specs=(P("row", "col"),), out_specs=P("row", "col"), check_vma=False)
```

time: 108 us -> 95.1 us (0.88)
  the two profiles are of different devices: /device:TPU:28 before, /device:TPU:26 now
where the time goes in v1:
time: 95.1 us; the launch traced here: 94.6 us
  Pallas kernels  94.6 us (99%)
    pallas_call x1, Pallas kernels, on_device(): pl.pallas_call(functools.partial(step_kernel, n_row, n_col), out_shape=ja...  90 us
    pallas_call x1, Pallas kernels, flush(): pl.pallas_call(flush_kernel, out_shape=jax.ShapeDtypeStruct(ready.shape,...  4.66 us

profile of v1, /device:TPU:26, one launch (start us, length us, event | category | flops | bytes accessed | tf_op | source)
XLA Modules:
  0.0 94.6 jit_solution(6236502046025767356)
XLA Ops:
  0.0 90.0 %whole_step.1.ready = f32[768,4096]{1,0:T(8,128)S(1)} custom-call(f32[768,4096]{1,0:T(8,128)} %matrix_ref.1), custom_call_target="tpu_custom_call" | custom-call | tf_op jit(solution)/shard_map/whole_step/pallas_call | solution.py:606
  90.0 4.7 %flush.1 = f32[768,4096]{1,0:T(8,128)} custom-call(f32[768,4096]{1,0:T(8,128)S(1)} %whole_step.1.ready), custom_call_target="tpu_custom_call" | custom-call | tf_op jit(solution)/shard_map/flush/pallas_call | solution.py:588

commit v2 on v1

--- a/solution.py
+++ b/solution.py
@@ -11,9 +11,12 @@
 STRIP = 8
 LANES = 128
 MESH = pl.DeviceIdType.MESH
-EARLY = 4
-MIX = 2
-END_LAG = 3
+EARLY = 8
+EARLY_UP = 4
+LATE = 3
+MIX = 4
+LEAD_PACE = 1.4
+HOP = 3.2
 
 
 def dot_exact(a, b, contract):
@@ -84,9 +87,53 @@
     return high, (x - high.astype(jnp.float32)).astype(jnp.bfloat16)
 
 
+def owned_counts(pairs):
+    return pairs - pairs // 3, pairs // 3
+
+
+def is_direct(i, owner):
+    return owner == 1 or i % MIX == MIX - 1
+
+
+def plan(role, counts):
+    events = []
+
+    def put(time, kind, owner, i):
+        events.append((time, len(events), (kind, owner, i)))
+
+    for i in range(counts[0]):
+        solved = max(36.5 + 0.4 * i, 25.5 + 1.5 * i)
+        sent = max(37.0 + 1.4 * i, solved)
+        if role == 0:
+            put(solved, "solve", 0, i)
+            if is_direct(i, 0):
+                put(sent + HOP, "pass", 0, i)
+        else:
+            put(sent + HOP * role, "own", 0, i)
+            if is_direct(i, 0):
+                put(sent + HOP * (role + 1), "other", 0, i)
+        if role in (1, 2):
+            put(18.3 + 1.5 * i + HOP * (2 - role), "down", 0, i)
+    for i in range(counts[1]):
+        solved = 32.6 + 2.75 * i
+        if role == 3:
+            put(solved, "solve", 1, i)
+            put(solved + HOP, "pass", 1, i)
+        else:
+            put(solved + HOP * (3 - role), "own", 1, i)
+            put(solved + HOP * (4 - role), "other", 1, i)
+        late = role == 2 and i == counts[1] - 1
+        if role in (1, 2):
+            put(36.5 if late else 13.0 + 2.8 * i + HOP * (role - 1), "up", 1, i)
+        if role == 2:
+            put(39.7 if late else 20.0 + 2.8 * i, "join", 1, i)
+    put(46.0, "sums", 0, 0)
+    return [event for _, _, event in sorted(events)]
+
+
 def step_kernel(
-    n_row, n_col, matrix_ref, updated,
-    partial, pair_in, chain_in, top_in, hold, stacked, shifted, panel, top, factor_ref, inverse_ref,
+    n_row, n_col, matrix_ref, updated, hold, shifted,
+    partial, pair_in, chain_in, top_in, stacked, panel, top, factor_ref, inverse_ref,
     parts, arrived, whole,
     fetch_sem, block_sem, own_sem,
     panel_send, panel_recv, part_send, part_recv, whole_send, whole_recv, top_send, top_recv, share_send, share_recv,
@@ -96,6 +143,9 @@
     row, col = lax.axis_index("row"), lax.axis_index("col")
     width = updated.shape[1]
     blocks = width // (4 * LANES)
+    pairs = 2 * blocks
+    counts = owned_counts(pairs)
+    prompt = pairs - LATE
     piece = PANEL // n_row
     outer_n = n_row // 2
     last = outer_n - 1
@@ -106,7 +156,6 @@
     is_end = first | final
     mine = jnp.where(first, 0, 1)
     near = jnp.where(2 * outer < outer_n, 0, 1)
-    far = 1 - near
     end_rows = [0, 1, n_row - 2, n_row - 1]
 
     barrier = pltpu.get_barrier_semaphore()
@@ -125,22 +174,35 @@
         place = lanes(j * (4 * LANES), 4 * LANES)
         return pltpu.make_async_copy(matrix_ref.at[:, place], updated.at[:, place], block_sem.at[j])
 
-    def scatter(i, e):
-        row_to = end_rows[e]
-        place = unit(2 * i + e // 2, e % 2)
+    def static_slot(i, owner):
+        return i + i // 2 if owner == 0 else 3 * i + 2
+
+    def owner_of(p):
+        return jnp.where(lax.rem(p, 3) == 2, 1, 0)
+
+    def turn_of(p):
+        return jnp.where(lax.rem(p, 3) == 2, lax.div(p, 3), p - lax.div(p, 3))
+
+    def scatter(p, side, up):
         return send(
-            matrix_ref.at[pl.ds(0, PANEL), place], top_in.at[i], scatter_send.at[i, e], scatter_recv.at[i],
-            {"row": row_to},
+            matrix_ref.at[pl.ds(0, PANEL), unit(p, side)], top_in.at[turn_of(p)],
+            scatter_send.at[p, side], scatter_recv.at[turn_of(p)], {"row": end_rows[2 * up + side]},
         )
 
     def keep(i):
-        return pltpu.make_async_copy(matrix_ref.at[pl.ds(0, PANEL), unit(2 * i, 0)], top_in.at[i], own_sem.at[i])
-
-    def start_scatter(i):
+        place = unit(static_slot(i, 0), 0)
+        return pltpu.make_async_copy(matrix_ref.at[pl.ds(0, PANEL), place], top_in.at[i], own_sem.at[i])
+
+    def start_scatter(p):
+        @pl.when((row == 0) & (owner_of(p) == 0) & (p < prompt))
+        def _():
+            scatter(p, 1, 0).start()
+
+    def start_up(i):
         @pl.when(row == 0)
         def _():
-            for e in range(1, 4):
-                scatter(i, e).start()
+            for side in range(2):
+                scatter(static_slot(i, 1), side, 1).start()
 
     def pair(p):
         return send(partial.at[:, unit(p, other)], pair_in.at[p], pair_send.at[p], pair_recv.at[p], partner)
@@ -152,17 +214,10 @@
             chain_send.at[p, slot], chain_recv.at[p, slot], {"row": row + 2 * (2 * towards - 1)},
         )
 
-    def is_direct(i, owner):
-        return (owner == 1) & (lax.rem(i, MIX) != 0)
-
-    def joins(owner):
-        return outer == jnp.where(owner == 0, 1, last - 1)
-
-    def owns(owner):
-        return is_end & (owner == mine)
-
-    def leads(owner):
-        return is_end & (owner != mine)
+    joins = outer == last - 1
+
+    def is_held(p):
+        return (owner_of(p) == 0) & (p >= prompt)
 
     def give(p):
         place = unit(p, inner)
@@ -187,18 +242,23 @@
         rest = jnp.dot(stacked[:PANEL], low, preferred_element_type=jnp.float32)
         partial[:, place] = both[:PANEL] + both[PANEL:] + rest
 
-    def exchange(i):
-        for side in range(2):
-            p = 2 * i + side
-
-            @pl.when(owns(side))
-            def _():
-                pair(p).start()
-
-            @pl.when(leads(side))
-            def _():
-                chain(p, side, True).start()
-                chain(p, side, False).start()
+    def exchange(p):
+        owner = owner_of(p)
+
+        @pl.when((owner == 0) & jnp.logical_not((row == 0) & is_held(p)))
+        def _():
+            pair(p).start()
+
+        @pl.when((owner == 1) & first)
+        def _():
+            chain(p, owner, True).start()
+            chain(p, owner, False).start()
+
+    def exchange_last():
+        @pl.when(final)
+        def _():
+            for i in range(counts[1]):
+                pair(static_slot(i, 1)).start()
 
     def prepare():
         high, low = split(panel[...])
@@ -213,11 +273,12 @@
         def _(j):
             load(j).wait()
             multiply(j)
-            exchange(j)
-
-            @pl.when(j + ahead < blocks)
-            def _():
-                start_scatter(j + ahead)
+            for p in (2 * j, 2 * j + 1):
+                exchange(p)
+
+                @pl.when(p + ahead < pairs)
+                def _():
+                    start_scatter(p + ahead)
 
     @pl.when(col == 0)
     def _():
@@ -237,8 +298,9 @@
 
     @pl.when(row == 0)
     def _():
-        for i in range(blocks):
-            keep(i).start()
+        for i in range(counts[0]):
+            if static_slot(i, 0) < prompt:
+                keep(i).start()
 
     pl.semaphore_wait(barrier, n_row - 1 + n_col - 1)
 
@@ -293,10 +355,11 @@
 
         panel_copy(heads[0], 0).start()
 
-        @pl.loop(0, blocks // 2)
-        def _(j):
-            exchange(j)
-            start_scatter(j)
+        @pl.loop(0, 2 * (blocks // 2))
+        def _(p):
+            exchange(p)
+
+            start_scatter(p)
 
         @pl.when(is_end)
         def _():
@@ -308,6 +371,9 @@
                 share(c, 0).start()
 
         multiply_range(blocks // 2, blocks, 0)
+        exchange_last()
+        for i in range(counts[1]):
+            start_up(i)
 
         @pl.when(is_end)
         def _():
@@ -337,10 +403,13 @@
 
     @pl.when(col != 0)
     def _():
-        for i in range(EARLY):
-            @pl.when(col != 1)
-            def _():
-                start_scatter(i)
+        @pl.when(col != 1)
+        def _():
+            for p in range(EARLY):
+                start_scatter(p)
+            for i in range(EARLY_UP):
+                start_up(i)
+
         root = {"col": 0}
         send(panel, panel, panel_send.at[0], panel_recv.at[0], root).wait_recv()
         relay = (lax.rem(col, 2) == 0) & (col + 1 < n_col)
@@ -352,6 +421,12 @@
         prepare()
         ahead = jnp.where(col == 1, 0, EARLY)
         multiply_range(0, blocks, ahead)
+        exchange_last()
+
+        for i in range(counts[1]):
+            @pl.when((col == 1) | (i >= EARLY_UP))
+            def _():
+                start_up(i)
 
         @pl.when(is_end)
         def _():
@@ -369,231 +444,232 @@
             total = total + term[...]
         partial[:, place] = total
 
-    def relay_sum(i, owner):
-        p = 2 * i + owner
-        chain(p, owner, True).wait_recv()
-        add(p, inner, chain_in.at[p, 0])
-
-        @pl.when(jnp.logical_not(joins(owner)))
-        def _():
-            chain(p, owner, True).start()
-
-        chain(p, owner, False).wait_recv()
-        add(p, other, chain_in.at[p, 1])
-
-        @pl.when(joins(owner))
-        def _():
-            pair(p).start()
-
-        @pl.when(jnp.logical_not(joins(owner)))
-        def _():
-            chain(p, owner, False).start()
-
-    def join_sum(i, owner):
-        @pl.when(joins(owner))
-        def _():
-            p = 2 * i + owner
+    def lead(i):
+        p = static_slot(i, 0)
+        pair(p).wait_recv()
+        add(p, inner, pair_in.at[p])
+        chain(p, 0, True).start()
+
+    def relay_down(i):
+        p = static_slot(i, 0)
+        pair(p).wait_recv()
+        chain(p, 0, True).wait_recv()
+        add(p, inner, pair_in.at[p], chain_in.at[p, 0])
+        chain(p, 0, True).start()
+
+    def relay_up(i):
+        p = static_slot(i, 1)
+        for own in (False, True):
+            chain(p, 1, own).wait_recv()
+            add(p, inner if own else other, chain_in.at[p, 0 if own else 1])
+
+            @pl.when(jnp.logical_not(joins))
+            def _():
+                chain(p, 1, own).start()
+
+            if not own:
+                @pl.when(joins)
+                def _():
+                    pair(p).start()
+
+    def join_up(i):
+        @pl.when(joins)
+        def _():
+            p = static_slot(i, 1)
             pair(p).wait_recv()
             add(p, inner, pair_in.at[p])
-            chain(p, owner, True).start()
+            chain(p, 1, True).start()
 
     @pl.when(is_end)
     def _():
         gram = jnp.concatenate([whole[q] for q in range(n_row)], axis=0)
 
-        factor, inverse = factor_values(gram, top[...])
+        strips = [2 + int(LEAD_PACE * i) for i in range(counts[0])]
+
+        def between(strip):
+            if strip in strips:
+                @pl.when(final)
+                def _():
+                    lead(strips.index(strip))
+
+        factor, inverse = factor_values(gram, top[...], between)
         factor_ref[...] = factor
         inverse_ref[:, :PANEL] = inverse
         inverse_ref[:, PANEL:] = dot_exact(inverse, factor, ((1,), (1,)))
 
+        @pl.when(final)
+        def _():
+            for i in range(counts[0]):
+                if strips[i] >= PANEL // STRIP:
+                    lead(i)
+
         @pl.when(row == 0)
         def _():
             high, low = split(panel[:PANEL] + factor)
             shifted[:PANEL, :PANEL] = high
             shifted[:PANEL, PANEL:] = low
 
-    @pl.when(jnp.logical_not(is_end))
-    def _():
-        @pl.loop(0, blocks + 2)
-        def _(s):
-            @pl.when(s >= 2)
+            for p in range(prompt, pairs):
+                if p % 3 != 2:
+                    place = lanes(p * (2 * LANES) + LANES, LANES)
+                    extra = dot_exact(factor, updated[:PANEL, place], ((0,), (0,)))
+                    partial[:, place] = partial[:, place] + extra
+                    pair(p).start()
+
+    def solve(i, owner):
+        p = static_slot(i, owner)
+        pair(p).wait_recv()
+        chain(p, owner, True).wait_recv()
+        place = unit(p, inner)
+        held = owner == 0 and p >= prompt
+
+        def at_row_zero():
+            if held:
+                top_in[i] = updated[:PANEL, place]
+            else:
+                keep(i).wait()
+
+        def elsewhere():
+            if held:
+                top_in[i] = jnp.zeros((PANEL, LANES), jnp.float32)
+            else:
+                send(top_in.at[i], top_in.at[i], scatter_send.at[0, 0], scatter_recv.at[i], {"row": 0}).wait_recv()
+
+        if owner == 0:
+            pl.when(row == 0)(at_row_zero)
+            pl.when(row != 0)(elsewhere)
+        else:
+            elsewhere()
+        total = partial[:, place] + pair_in[p] + chain_in[p, 0]
+        hold[:, place] = dot_exact(inverse_ref[...], jnp.concatenate([total, top_in[i]], axis=0), ((1,), (0,)))
+        onward(p, owner, True).start()
+        give(p).start()
+
+    def pass_other(i, owner):
+        p = static_slot(i, owner)
+        given(p).wait_recv()
+        onward(p, owner, False).start()
+
+    def accept(i, owner, own, stops):
+        p = static_slot(i, owner)
+        onward(p, owner, own).wait_recv()
+        if not stops:
+            onward(p, owner, own).start()
+        if own and not is_direct(i, owner):
+            give(p).start()
+
+    def settle_sums(role):
+        for p in range(pairs):
+            owner = 1 if p % 3 == 2 else 0
+            if owner == 0:
+                pair(p).wait_send()
+                if role != 0:
+                    chain(p, 0, True).wait_send()
+            elif role == 0:
+                chain(p, 1, True).wait_send()
+                chain(p, 1, False).wait_send()
+            elif role == 3:
+                pair(p).wait_send()
+            else:
+                chain(p, 1, True).wait_send()
+
+                @pl.when(joins)
+                def _():
+                    pair(p).wait_send()
+
+                @pl.when(jnp.logical_not(joins))
+                def _():
+                    chain(p, 1, False).wait_send()
+        if role == 0:
+            @pl.when(row == 0)
             def _():
-                join_sum(s - 2, near)
-
-            @pl.when(s < blocks)
-            def _():
-                relay_sum(s, far)
-
-            @pl.when((s >= 1) & (s <= blocks))
-            def _():
-                relay_sum(s - 1, near)
-
-    def update(p):
-        place = lanes(p * (2 * LANES), 2 * LANES)
-        high, low = split(hold[:, place])
+                for p in range(pairs):
+                    if p % 3 == 2:
+                        scatter(p, 0, 1).wait_send()
+                        scatter(p, 1, 1).wait_send()
+                    elif p < prompt:
+                        scatter(p, 1, 0).wait_send()
+
+    def settle_back(role):
+        for owner in range(2):
+            for i in range(counts[owner]):
+                p = static_slot(i, owner)
+                owned = role == (0, 3)[owner]
+                stops = role == (3, 0)[owner]
+                if owned or not is_direct(i, owner):
+                    give(p).wait_send()
+                if not is_direct(i, owner):
+                    given(p).wait_recv()
+                if not stops:
+                    onward(p, owner, True).wait_send()
+                    if is_direct(i, owner):
+                        onward(p, owner, False).wait_send()
+
+    def follow(role):
+        for event in plan(role, counts):
+            kind, owner, i = event
+            if kind == "solve":
+                solve(i, owner)
+            elif kind == "pass":
+                pass_other(i, owner)
+            elif kind == "down":
+                relay_down(i)
+            elif kind == "up":
+                relay_up(i)
+            elif kind == "join":
+                join_up(i)
+            elif kind == "sums":
+                settle_sums(role)
+            else:
+                accept(i, owner, kind == "own", role == (3, 0)[owner])
+        settle_back(role)
+
+    pl.when(first)(lambda: follow(0))
+    pl.when(jnp.logical_not(is_end) & (near == 0))(lambda: follow(1))
+    pl.when(jnp.logical_not(is_end) & (near == 1))(lambda: follow(2))
+    pl.when(final)(lambda: follow(3))
+
+
+def flush_kernel(block, hold, shifted, out, ring, sem):
+    slots = ring.shape[0]
+    pairs = out.shape[1] // (2 * LANES)
+
+    def lanes(p):
+        return pl.ds(pl.multiple_of(p * (2 * LANES), LANES), 2 * LANES)
+
+    def store(p):
+        slot = lax.rem(p, slots)
+        return pltpu.make_async_copy(ring.at[slot], out.at[:, lanes(p)], sem.at[slot])
+
+    @pl.loop(0, pairs)
+    def _(p):
+        @pl.when(p >= slots)
+        def _():
+            store(p - slots).wait()
+
+        high, low = split(hold[:, lanes(p)])
         both = jnp.dot(shifted[...], jnp.concatenate([high, high], axis=0), preferred_element_type=jnp.float32)
         rest = jnp.dot(shifted[:, :PANEL], low, preferred_element_type=jnp.float32)
-        updated[:, place] = updated[:, place] - (both + rest)
-
-    def solve(i):
-        p = 2 * i + mine
-        pair(p).wait_recv()
-        chain(p, mine, True).wait_recv()
-
-        @pl.when(row == 0)
-        def _():
-            keep(i).wait()
-
-        @pl.when(row != 0)
-        def _():
-            send(top_in.at[i], top_in.at[i], scatter_send.at[i, 0], scatter_recv.at[i], {"row": 0}).wait_recv()
-
-        place = unit(p, inner)
-        total = partial[:, place] + pair_in[p] + chain_in[p, 0]
-        hold[:, place] = dot_exact(inverse_ref[...], jnp.concatenate([total, top_in[i]], axis=0), ((1,), (0,)))
-        onward(p, mine, True).start()
-        give(p).start()
-
-    def pass_other(i):
-        p = 2 * i + mine
-
-        @pl.when(is_direct(i, mine))
-        def _():
-            given(p).wait_recv()
-            onward(p, mine, False).start()
-
-    def accept(i, owner):
-        p = 2 * i + owner
-        stops = jnp.where(owner == 0, final, first)
-        onward(p, owner, True).wait_recv()
-
-        @pl.when(jnp.logical_not(stops))
-        def _():
-            onward(p, owner, True).start()
-
-        @pl.when(is_direct(i, owner))
-        def _():
-            onward(p, owner, False).wait_recv()
-
-            @pl.when(jnp.logical_not(stops))
-            def _():
-                onward(p, owner, False).start()
-
-        @pl.when(jnp.logical_not(is_direct(i, owner)))
-        def _():
-            give(p).start()
-
-    def finish(i, owner):
-        p = 2 * i + owner
-
-        @pl.when(jnp.logical_not(is_direct(i, owner)))
-        def _():
-            given(p).wait_recv()
-
-        update(p)
-
-    @pl.when(is_end)
-    def _():
-        @pl.loop(0, blocks + 2)
-        def _(i):
-            @pl.when(i < blocks)
-            def _():
-                solve(i)
-
-            @pl.when(i >= 2)
-            def _():
-                pass_other(i - 2)
-
-    def settle_sums(i, side):
-        p = 2 * i + side
-
-        @pl.when(owns(side) | joins(side))
-        def _():
-            pair(p).wait_send()
-
-        @pl.when(jnp.logical_not(owns(side)))
-        def _():
-            chain(p, side, True).wait_send()
-
-        @pl.when(jnp.logical_not(owns(side) | joins(side)))
-        def _():
-            chain(p, side, False).wait_send()
-
-    def settle_back(i, side):
-        p = 2 * i + side
-
-        @pl.when(jnp.logical_not(leads(side)))
-        def _():
-            onward(p, side, True).wait_send()
-
-            @pl.when(is_direct(i, side))
-            def _():
-                onward(p, side, False).wait_send()
-
-        @pl.when(owns(side) | jnp.logical_not(is_direct(i, side)))
-        def _():
-            give(p).wait_send()
-
-    wait = jnp.where(is_end, 0, 2)
-    lag = jnp.where(is_end, END_LAG, 1)
-
-    @pl.loop(0, blocks + END_LAG + 2)
-    def _(s):
-        @pl.when(s < blocks)
-        def _():
-            for side in range(2):
-                settle_sums(s, side)
-
-            @pl.when(row == 0)
-            def _():
-                for e in range(1, 4):
-                    scatter(s, e).wait_send()
-
-        @pl.when((s >= wait) & (s < blocks + wait))
-        def _():
-            finish(s - wait, near)
-
-        @pl.when(jnp.logical_not(is_end) & (s < blocks))
-        def _():
-            accept(s, near)
-
-        @pl.when((s >= lag + 2) & (s < blocks + lag + 2))
-        def _():
-            finish(s - lag - 2, far)
-
-        @pl.when((s >= lag) & (s < blocks + lag))
-        def _():
-            accept(s - lag, far)
-
-    @pl.loop(0, blocks)
-    def _(i):
-        for side in range(2):
-            settle_back(i, side)
-
-
-def flush_kernel(ready, out, sem):
-    pieces = sem.shape[0]
-    rows = out.shape[0] // pieces
-    copies = [
-        pltpu.make_async_copy(ready.at[pl.ds(q * rows, rows)], out.at[pl.ds(q * rows, rows)], sem.at[q])
-        for q in range(pieces)
-    ]
-    for copy in copies:
-        copy.start()
-    for copy in copies:
-        copy.wait()
-
-
-def flush(ready):
+        ring[lax.rem(p, slots)] = block[:, lanes(p)] - (both + rest)
+        store(p).start()
+
+    @pl.loop(pairs - slots, pairs)
+    def _(p):
+        store(p).wait()
+
+
+def flush(block, hold, shifted):
+    height, width = block.shape
+    vmem = pl.BlockSpec(memory_space=pltpu.VMEM)
     return pl.pallas_call(
         flush_kernel,
-        out_shape=jax.ShapeDtypeStruct(ready.shape, ready.dtype),
-        in_specs=[pl.BlockSpec(memory_space=pltpu.VMEM)],
+        out_shape=jax.ShapeDtypeStruct(block.shape, block.dtype),
+        in_specs=[vmem] * 3,
         out_specs=pl.BlockSpec(memory_space=pl.ANY),
-        scratch_shapes=[pltpu.SemaphoreType.DMA((8,))],
+        scratch_shapes=[pltpu.VMEM((4, height, 2 * LANES), jnp.float32), pltpu.SemaphoreType.DMA((4,))],
         compiler_params=pltpu.CompilerParams(vmem_limit_bytes=16 * 1024 * 1024),
         name="flush",
-    )(ready)
+    )(block, hold, shifted)
 
 
 def on_device(n_row, n_col, matrix):
@@ -601,21 +677,24 @@
     piece = PANEL // n_row
     blocks = width // (4 * LANES)
     pairs = 2 * blocks
+    most = owned_counts(pairs)[0]
     dma = pltpu.SemaphoreType.DMA
     f32, bf16 = jnp.float32, jnp.bfloat16
-    ready = pl.pallas_call(
+    parts = pl.pallas_call(
         functools.partial(step_kernel, n_row, n_col),
-        out_shape=jax.ShapeDtypeStruct((height, width), f32),
+        out_shape=(
+            jax.ShapeDtypeStruct((height, width), f32),
+            jax.ShapeDtypeStruct((PANEL, width), f32),
+            jax.ShapeDtypeStruct((height, 2 * PANEL), bf16),
+        ),
         in_specs=[pl.BlockSpec(memory_space=pl.ANY)],
-        out_specs=pl.BlockSpec(memory_space=pltpu.VMEM),
+        out_specs=(pl.BlockSpec(memory_space=pltpu.VMEM),) * 3,
         scratch_shapes=[
             pltpu.VMEM((PANEL, width), f32),
             pltpu.VMEM((pairs, PANEL, LANES), f32),
             pltpu.VMEM((pairs, 2, PANEL, LANES), f32),
-            pltpu.VMEM((blocks, PANEL, LANES), f32),
-            pltpu.VMEM((PANEL, width), f32),
+            pltpu.VMEM((most, PANEL, LANES), f32),
             pltpu.VMEM((2 * PANEL, height), bf16),
-            pltpu.VMEM((height, 2 * PANEL), bf16),
             pltpu.VMEM((height, PANEL), f32),
             pltpu.VMEM((PANEL, PANEL), f32),
             pltpu.VMEM((PANEL, PANEL), f32),
@@ -625,7 +704,7 @@
             pltpu.VMEM((n_row, piece, PANEL), f32),
             dma((1,)),
             dma((blocks,)),
-            dma((blocks,)),
+            dma((most,)),
             dma((n_col,)),
             dma((1,)),
             dma((n_row - 1,)),
@@ -636,8 +715,8 @@
             dma((1,)),
             dma((n_col - 1, 2)),
             dma((2,)),
-            dma((blocks, 4)),
-            dma((blocks,)),
+            dma((pairs, 2)),
+            dma((most,)),
             dma((pairs,)),
             dma((pairs,)),
             dma((pairs, 2)),
@@ -648,11 +727,11 @@
             dma((pairs, 2)),
         ],
         compiler_params=pltpu.CompilerParams(
-            collective_id=0, has_side_effects=True, vmem_limit_bytes=40 * 1024 * 1024
+            collective_id=0, has_side_effects=True, vmem_limit_bytes=36 * 1024 * 1024
         ),
         name="whole_step",
     )(matrix)
-    return flush(ready)
+    return flush(*parts)
 
 
 def solution(mesh):

time: 95.1 us -> 84 us (0.88)
  the two profiles are of different devices: /device:TPU:26 before, /device:TPU:28 now
where the time goes in v2:
time: 84 us; the launch traced here: 83.8 us
  Pallas kernels  83.6 us (100%)
    pallas_call x1, Pallas kernels, on_device(): pl.pallas_call(functools.partial(step_kernel, n_row, n_col), out_shape=(j...  76.9 us
    pallas_call x1, Pallas kernels, flush(): pl.pallas_call(flush_kernel, out_shape=jax.ShapeDtypeStruct(block.shape,...  6.77 us

profile of v2, /device:TPU:28, one launch (start us, length us, event | category | flops | bytes accessed | tf_op | source)
XLA Modules:
  0.0 83.8 jit_solution(11075730696001915403)
XLA Ops:
  0.0 76.9 %whole_step.1 = (f32[768,4096]{1,0:T(8,128)S(1)}, f32[128,4096]{1,0:T(8,128)S(1)}, bf16[768,256]{1,0:T(8,128)(2,1)S(1)}) custom-call(f32[768,4096]{1,0:T(8,128)} %matrix_ref.1), custom_call_target="tpu_custom_call" | custom-call | tf_op jit(solution)/shard_map/whole_step/pallas_call | solution.py:683
  76.9 6.8 %flush.1 = f32[768,4096]{1,0:T(8,128)} custom-call(f32[768,4096]{1,0:T(8,128)S(1)} %get-tuple-element.8.block, f32[128,4096]{1,0:T(8,128)S(1)} %get-tuple-element.9.hold, bf16[768,256]{1,0:T(8,128)(2,1)S(1)} %get-tuple-element.10.shifted), custom_call_target="tpu_custom_call" | custom-call | tf_op jit(solution)/shard_map/flush/pallas_call | solution.py:664

commit v3 on v2

--- a/solution.py
+++ b/solution.py
@@ -12,11 +12,10 @@
 LANES = 128
 MESH = pl.DeviceIdType.MESH
 EARLY = 8
-EARLY_UP = 4
-LATE = 3
-MIX = 4
-LEAD_PACE = 1.4
-HOP = 3.2
+LATE = 7
+UP_SHARE = 4
+LEAD_PACE = 2.5
+HOP = 3.5
 
 
 def dot_exact(a, b, contract):
@@ -27,43 +26,59 @@
 
 def factor_values(gram, top, between=lambda strip: None):
     strips = PANEL // STRIP
-    rows = lax.broadcasted_iota(jnp.int32, (STRIP, 1), 0)
+    shape = (STRIP, LANES)
+    rows = lax.broadcasted_iota(jnp.int32, shape, 0)
+    lanes = lax.broadcasted_iota(jnp.int32, shape, 1)
     eye = (
         lax.broadcasted_iota(jnp.int32, (PANEL, PANEL), 0) == lax.broadcasted_iota(jnp.int32, (PANEL, PANEL), 1)
     ).astype(jnp.float32)
     chol = jnp.concatenate([gram, eye], axis=1)
     work = jnp.concatenate([top, jnp.zeros_like(top)], axis=1)
     factor_rows = []
-    lanes = lax.broadcasted_iota(jnp.int32, (STRIP, 2 * PANEL), 1)
     previous = None
+
+    def spread(x, start):
+        return [jnp.broadcast_to(x[:, start + c : start + c + 1], shape) for c in range(STRIP)]
+
     for strip in range(strips + 1):
         at, back = strip * STRIP, (strip - 1) * STRIP
         if strip < strips:
             between(strip)
             panel = chol[:STRIP]
-            scale = jnp.ones((STRIP, 1), jnp.float32)
+            columns = spread(panel, at)
+            halves = [panel[:, :LANES], panel[:, LANES:]]
+            scale = jnp.ones(shape, jnp.float32)
         if strip > 0:
             inner = work[back : back + STRIP] + previous
             aside = work[:, back : back + STRIP]
+            inner_columns = spread(inner, back)
+            inner_halves = [inner[:, :LANES], inner[:, LANES:]]
         for j in range(STRIP):
             if strip < strips:
-                column = panel[:, at + j : at + j + 1]
-                pivot = column[j : j + 1]
-                multiplier = jnp.where(rows > j, column / pivot, 0.0)
+                pivot = columns[j][j : j + 1]
+                multiplier = jnp.where(rows > j, columns[j] * (1.0 / pivot), 0.0)
+                scale = jnp.where(rows == j, lax.rsqrt(pivot), scale)
+                columns = [x if c <= j else x - multiplier * x[j : j + 1] for c, x in enumerate(columns)]
+                halves = [x - multiplier * x[j : j + 1] for x in halves]
             if strip > 0:
-                inner_column = inner[:, back + j : back + j + 1]
-                pivot_row = inner[j : j + 1] / inner_column[j : j + 1]
-            if strip < strips:
-                scale = jnp.where(rows == j, lax.rsqrt(pivot), scale)
-                panel = panel - multiplier * panel[j : j + 1]
-            if strip > 0:
-                inner = jnp.where(rows == j, pivot_row, inner - inner_column * pivot_row)
+                column = inner_columns[j]
+                inverse = 1.0 / column[j : j + 1]
+
+                def eliminate(x):
+                    pivot_row = x[j : j + 1] * inverse
+                    return jnp.where(rows == j, pivot_row, x - column * pivot_row)
+
+                inner_columns = [x if c <= j else eliminate(x) for c, x in enumerate(inner_columns)]
+                inner_halves = [eliminate(x) for x in inner_halves]
         if strip < strips:
-            panel = jnp.where(lanes >= at + rows, panel * scale, 0.0)
-            factor_rows.append(panel[:, :PANEL])
+            halves = [halves[0] * scale, halves[1] * scale]
+            halves[0] = jnp.where(lanes >= at + rows, halves[0], 0.0)
+            panel = jnp.concatenate(halves, axis=1)
+            factor_rows.append(halves[0])
             if strip < strips - 1:
                 chol = chol[STRIP:] - dot_exact(panel[:, at + STRIP : PANEL], panel, ((0,), (0,)))
         if strip > 0:
+            inner = jnp.concatenate(inner_halves, axis=1)
             update = dot_exact(aside, inner, ((1,), (0,)))
             pieces = []
             if back > 0:
@@ -88,52 +103,63 @@
 
 
 def owned_counts(pairs):
-    return pairs - pairs // 3, pairs // 3
+    return pairs - pairs // UP_SHARE, pairs // UP_SHARE
+
+
+def slot_of(i, owner, n_up):
+    if owner == 1:
+        return 2 * i + 1
+    return 2 * i if i < n_up else i + n_up
 
 
 def is_direct(i, owner):
-    return owner == 1 or i % MIX == MIX - 1
-
-
-def plan(role, counts):
+    return owner == 1
+
+
+def plan(role, counts, prompt):
     events = []
 
     def put(time, kind, owner, i):
         events.append((time, len(events), (kind, owner, i)))
 
-    for i in range(counts[0]):
-        solved = max(36.5 + 0.4 * i, 25.5 + 1.5 * i)
-        sent = max(37.0 + 1.4 * i, solved)
-        if role == 0:
-            put(solved, "solve", 0, i)
-            if is_direct(i, 0):
-                put(sent + HOP, "pass", 0, i)
-        else:
-            put(sent + HOP * role, "own", 0, i)
-            if is_direct(i, 0):
-                put(sent + HOP * (role + 1), "other", 0, i)
-        if role in (1, 2):
-            put(18.3 + 1.5 * i + HOP * (2 - role), "down", 0, i)
-    for i in range(counts[1]):
-        solved = 32.6 + 2.75 * i
+    held = [0, 0]
+    turns = sorted((slot_of(i, owner, counts[1]), owner, i) for owner in range(2) for i in range(counts[owner]))
+    for p, owner, i in turns:
+        after = held[owner]
+        if p >= prompt:
+            held[owner] += 1
+            if role == 0:
+                put(26.0 + 0.1 * i if owner == 1 else 27.0 + 0.7 * after, "late", owner, i)
+        if owner == 0:
+            sent = 30.7 + 1.7 * i
+            if role == 0:
+                put(27.3 + 0.7 * i, "solve", 0, i)
+            else:
+                put(sent + HOP * role, "own", 0, i)
+            if role in (1, 2):
+                put(21.2 + 1.4 * i + 3.2 * (2 - role), "down", 0, i)
+            continue
+        near, away, join, solved = 25.0 + 2.8 * i, 29.0 + 2.8 * i, 33.0 + 2.8 * i, 37.0 + 2.8 * i
+        if p >= prompt:
+            near, away, join, solved = 34.0 + 3.5 * after, 37.5 + 3.5 * after, 41.0 + 3.5 * after, 46.0 + 3.0 * after
         if role == 3:
             put(solved, "solve", 1, i)
             put(solved + HOP, "pass", 1, i)
         else:
             put(solved + HOP * (3 - role), "own", 1, i)
             put(solved + HOP * (4 - role), "other", 1, i)
-        late = role == 2 and i == counts[1] - 1
-        if role in (1, 2):
-            put(36.5 if late else 13.0 + 2.8 * i + HOP * (role - 1), "up", 1, i)
+        if role == 1:
+            put(near, "up", 1, i)
         if role == 2:
-            put(39.7 if late else 20.0 + 2.8 * i, "join", 1, i)
-    put(46.0, "sums", 0, 0)
+            put(away, "up", 1, i)
+            put(join, "join", 1, i)
+    put(99.0, "sums", 0, 0)
     return [event for _, _, event in sorted(events)]
 
 
 def step_kernel(
-    n_row, n_col, matrix_ref, updated, hold, shifted,
-    partial, pair_in, chain_in, top_in, stacked, panel, top, factor_ref, inverse_ref,
+    n_row, n_col, matrix_ref, hold, shifted,
+    block, partial, pair_in, chain_in, top_in, stacked, panel, top, factor_ref, inverse_ref,
     parts, arrived, whole,
     fetch_sem, block_sem, own_sem,
     panel_send, panel_recv, part_send, part_recv, whole_send, whole_recv, top_send, top_recv, share_send, share_recv,
@@ -141,7 +167,7 @@
     give_send, give_recv, pass_send, pass_recv,
 ):
     row, col = lax.axis_index("row"), lax.axis_index("col")
-    width = updated.shape[1]
+    width = block.shape[1]
     blocks = width // (4 * LANES)
     pairs = 2 * blocks
     counts = owned_counts(pairs)
@@ -172,16 +198,16 @@
 
     def load(j):
         place = lanes(j * (4 * LANES), 4 * LANES)
-        return pltpu.make_async_copy(matrix_ref.at[:, place], updated.at[:, place], block_sem.at[j])
+        return pltpu.make_async_copy(matrix_ref.at[:, place], block.at[:, place], block_sem.at[j])
 
     def static_slot(i, owner):
-        return i + i // 2 if owner == 0 else 3 * i + 2
+        return slot_of(i, owner, counts[1])
 
     def owner_of(p):
-        return jnp.where(lax.rem(p, 3) == 2, 1, 0)
+        return jnp.where((p < 2 * counts[1]) & (lax.rem(p, 2) == 1), 1, 0)
 
     def turn_of(p):
-        return jnp.where(lax.rem(p, 3) == 2, lax.div(p, 3), p - lax.div(p, 3))
+        return jnp.where(p < 2 * counts[1], lax.div(p, 2), p - counts[1])
 
     def scatter(p, side, up):
         return send(
@@ -199,7 +225,7 @@
             scatter(p, 1, 0).start()
 
     def start_up(i):
-        @pl.when(row == 0)
+        @pl.when((row == 0) & (static_slot(i, 1) < prompt))
         def _():
             for side in range(2):
                 scatter(static_slot(i, 1), side, 1).start()
@@ -215,9 +241,6 @@
         )
 
     joins = outer == last - 1
-
-    def is_held(p):
-        return (owner_of(p) == 0) & (p >= prompt)
 
     def give(p):
         place = unit(p, inner)
@@ -237,7 +260,7 @@
 
     def multiply(j):
         place = lanes(j * (4 * LANES), 4 * LANES)
-        high, low = split(updated[:, place])
+        high, low = split(block[:, place])
         both = jnp.dot(stacked[...], high, preferred_element_type=jnp.float32)
         rest = jnp.dot(stacked[:PANEL], low, preferred_element_type=jnp.float32)
         partial[:, place] = both[:PANEL] + both[PANEL:] + rest
@@ -245,11 +268,13 @@
     def exchange(p):
         owner = owner_of(p)
 
-        @pl.when((owner == 0) & jnp.logical_not((row == 0) & is_held(p)))
+        prompt_here = jnp.logical_not((row == 0) & (p >= prompt))
+
+        @pl.when((owner == 0) & prompt_here)
         def _():
             pair(p).start()
 
-        @pl.when((owner == 1) & first)
+        @pl.when((owner == 1) & first & prompt_here)
         def _():
             chain(p, owner, True).start()
             chain(p, owner, False).start()
@@ -354,6 +379,8 @@
                 whole_copy(e).start()
 
         panel_copy(heads[0], 0).start()
+        for i in range(counts[1]):
+            start_up(i)
 
         @pl.loop(0, 2 * (blocks // 2))
         def _(p):
@@ -372,8 +399,6 @@
 
         multiply_range(blocks // 2, blocks, 0)
         exchange_last()
-        for i in range(counts[1]):
-            start_up(i)
 
         @pl.when(is_end)
         def _():
@@ -407,7 +432,7 @@
         def _():
             for p in range(EARLY):
                 start_scatter(p)
-            for i in range(EARLY_UP):
+            for i in range(counts[1]):
                 start_up(i)
 
         root = {"col": 0}
@@ -417,16 +442,16 @@
         @pl.when(relay)
         def _():
             panel_copy(col + 1, 0).start()
+
+        @pl.when(col == 1)
+        def _():
+            for i in range(counts[1]):
+                start_up(i)
 
         prepare()
         ahead = jnp.where(col == 1, 0, EARLY)
         multiply_range(0, blocks, ahead)
         exchange_last()
-
-        for i in range(counts[1]):
-            @pl.when((col == 1) | (i >= EARLY_UP))
-            def _():
-                start_up(i)
 
         @pl.when(is_end)
         def _():
@@ -509,23 +534,30 @@
             shifted[:PANEL, :PANEL] = high
             shifted[:PANEL, PANEL:] = low
 
-            for p in range(prompt, pairs):
-                if p % 3 != 2:
-                    place = lanes(p * (2 * LANES) + LANES, LANES)
-                    extra = dot_exact(factor, updated[:PANEL, place], ((0,), (0,)))
-                    partial[:, place] = partial[:, place] + extra
-                    pair(p).start()
+    def late(i, owner):
+        p = static_slot(i, owner)
+
+        @pl.when(row == 0)
+        def _():
+            place = unit(p, 1) if owner == 0 else lanes(p * (2 * LANES), 2 * LANES)
+            extra = dot_exact(factor_ref[...], block[:PANEL, place], ((0,), (0,)))
+            partial[:, place] = partial[:, place] + extra
+            if owner == 0:
+                pair(p).start()
+            else:
+                chain(p, 1, True).start()
+                chain(p, 1, False).start()
 
     def solve(i, owner):
         p = static_slot(i, owner)
         pair(p).wait_recv()
         chain(p, owner, True).wait_recv()
         place = unit(p, inner)
-        held = owner == 0 and p >= prompt
+        held = p >= prompt
 
         def at_row_zero():
             if held:
-                top_in[i] = updated[:PANEL, place]
+                top_in[i] = block[:PANEL, place]
             else:
                 keep(i).wait()
 
@@ -558,9 +590,10 @@
         if own and not is_direct(i, owner):
             give(p).start()
 
+    turns = sorted((static_slot(i, owner), owner, i) for owner in range(2) for i in range(counts[owner]))
+
     def settle_sums(role):
-        for p in range(pairs):
-            owner = 1 if p % 3 == 2 else 0
+        for p, owner, _ in turns:
             if owner == 0:
                 pair(p).wait_send()
                 if role != 0:
@@ -583,8 +616,8 @@
         if role == 0:
             @pl.when(row == 0)
             def _():
-                for p in range(pairs):
-                    if p % 3 == 2:
+                for p, owner, _ in turns:
+                    if owner == 1 and p < prompt:
                         scatter(p, 0, 1).wait_send()
                         scatter(p, 1, 1).wait_send()
                     elif p < prompt:
@@ -606,10 +639,12 @@
                         onward(p, owner, False).wait_send()
 
     def follow(role):
-        for event in plan(role, counts):
+        for event in plan(role, counts, prompt):
             kind, owner, i = event
             if kind == "solve":
                 solve(i, owner)
+            elif kind == "late":
+                late(i, owner)
             elif kind == "pass":
                 pass_other(i, owner)
             elif kind == "down":
@@ -680,16 +715,16 @@
     most = owned_counts(pairs)[0]
     dma = pltpu.SemaphoreType.DMA
     f32, bf16 = jnp.float32, jnp.bfloat16
-    parts = pl.pallas_call(
+    hold, shifted = pl.pallas_call(
         functools.partial(step_kernel, n_row, n_col),
         out_shape=(
-            jax.ShapeDtypeStruct((height, width), f32),
             jax.ShapeDtypeStruct((PANEL, width), f32),
             jax.ShapeDtypeStruct((height, 2 * PANEL), bf16),
         ),
-        in_specs=[pl.BlockSpec(memory_space=pl.ANY)],
-        out_specs=(pl.BlockSpec(memory_space=pltpu.VMEM),) * 3,
+        in_specs=[pl.BlockSpec(memory_space=pltpu.HBM)],
+        out_specs=(pl.BlockSpec(memory_space=pltpu.VMEM),) * 2,
         scratch_shapes=[
+            pltpu.VMEM((height, width), f32),
             pltpu.VMEM((PANEL, width), f32),
             pltpu.VMEM((pairs, PANEL, LANES), f32),
             pltpu.VMEM((pairs, 2, PANEL, LANES), f32),
@@ -727,11 +762,11 @@
             dma((pairs, 2)),
         ],
         compiler_params=pltpu.CompilerParams(
-            collective_id=0, has_side_effects=True, vmem_limit_bytes=36 * 1024 * 1024
+            collective_id=0, has_side_effects=True, vmem_limit_bytes=44 * 1024 * 1024
         ),
         name="whole_step",
     )(matrix)
-    return flush(*parts)
+    return flush(matrix, hold, shifted)
 
 
 def solution(mesh):

time: 84 us -> 75.1 us (0.89)
  the two profiles are of different devices: /device:TPU:28 before, /device:TPU:26 now
where the time goes in v3:
time: 75.1 us; the launch traced here: 75 us
  Pallas kernels  74.8 us (100%)
    pallas_call x1, Pallas kernels, on_device(): pl.pallas_call(functools.partial(step_kernel, n_row, n_col), out_shape=(j...  68 us
    pallas_call x1, Pallas kernels, flush(): pl.pallas_call(flush_kernel, out_shape=jax.ShapeDtypeStruct(block.shape,...  6.77 us

profile of v3, /device:TPU:26, one launch (start us, length us, event | category | flops | bytes accessed | tf_op | source)
XLA Modules:
  0.0 75.0 jit_solution(4742150102872859634)
XLA Ops:
  0.0 0.0 copy-start
  0.0 68.0 %whole_step.1 = (f32[128,4096]{1,0:T(8,128)S(1)}, bf16[768,256]{1,0:T(8,128)(2,1)S(1)}) custom-call(f32[768,4096]{1,0:T(8,128)} %block.1), custom_call_target="tpu_custom_call" | custom-call | tf_op jit(solution)/shard_map/whole_step/pallas_call | solution.py:718
  68.1 0.0 copy-done
  68.1 6.8 %flush.1 = f32[768,4096]{1,0:T(8,128)} custom-call(f32[768,4096]{1,0:T(8,128)S(1)} %copy-done, f32[128,4096]{1,0:T(8,128)S(1)} %get-tuple-element.7.hold, bf16[768,256]{1,0:T(8,128)(2,1)S(1)} %get-tuple-element.8.shifted), custom_call_target="tpu_custom_call" | custom-call | tf_op jit(solution)/shard_map/flush/pallas_call | solution.py:699
Async XLA Ops:
  0.0 68.1 %copy-start = (f32[768,4096]{1,0:T(8,128)S(1)}, f32[768,4096]{1,0:T(8,128)}, u32[]{:S(2)}) copy-start(f32[768,4096]{1,0:T(8,128)} %block.1) | copy-start | bytes 37748740

commit v4 on v3

--- a/solution.py
+++ b/solution.py
@@ -15,7 +15,7 @@
 LATE = 7
 UP_SHARE = 4
 LEAD_PACE = 2.5
-HOP = 3.5
+HOP = 4.1
 
 
 def dot_exact(a, b, contract):
@@ -131,7 +131,7 @@
             if role == 0:
                 put(26.0 + 0.1 * i if owner == 1 else 27.0 + 0.7 * after, "late", owner, i)
         if owner == 0:
-            sent = 30.7 + 1.7 * i
+            sent = 31.4 + 1.5 * i
             if role == 0:
                 put(27.3 + 0.7 * i, "solve", 0, i)
             else:
@@ -139,21 +139,20 @@
             if role in (1, 2):
                 put(21.2 + 1.4 * i + 3.2 * (2 - role), "down", 0, i)
             continue
-        near, away, join, solved = 25.0 + 2.8 * i, 29.0 + 2.8 * i, 33.0 + 2.8 * i, 37.0 + 2.8 * i
+        near, away, join, solved = 25.0 + 2.8 * i, 29.0 + 2.8 * i, 33.0 + 2.8 * i, 37.0 + 2.4 * i
         if p >= prompt:
             near, away, join, solved = 34.0 + 3.5 * after, 37.5 + 3.5 * after, 41.0 + 3.5 * after, 46.0 + 3.0 * after
         if role == 3:
             put(solved, "solve", 1, i)
-            put(solved + HOP, "pass", 1, i)
+            put(solved + 4.5, "pass", 1, i)
         else:
-            put(solved + HOP * (3 - role), "own", 1, i)
-            put(solved + HOP * (4 - role), "other", 1, i)
+            put(solved + 1.5 + HOP * (3 - role), "own", 1, i)
+            put(solved + 2.0 + HOP * (4 - role), "other", 1, i)
         if role == 1:
             put(near, "up", 1, i)
         if role == 2:
             put(away, "up", 1, i)
             put(join, "join", 1, i)
-    put(99.0, "sums", 0, 0)
     return [event for _, _, event in sorted(events)]
 
 
@@ -207,17 +206,19 @@
         return jnp.where((p < 2 * counts[1]) & (lax.rem(p, 2) == 1), 1, 0)
 
     def turn_of(p):
+        if isinstance(p, int):
+            return p // 2 if p < 2 * counts[1] else p - counts[1]
         return jnp.where(p < 2 * counts[1], lax.div(p, 2), p - counts[1])
 
     def scatter(p, side, up):
         return send(
             matrix_ref.at[pl.ds(0, PANEL), unit(p, side)], top_in.at[turn_of(p)],
-            scatter_send.at[p, side], scatter_recv.at[turn_of(p)], {"row": end_rows[2 * up + side]},
+            scatter_send.at[0], scatter_recv.at[turn_of(p)], {"row": end_rows[2 * up + side]},
         )
 
     def keep(i):
         place = unit(static_slot(i, 0), 0)
-        return pltpu.make_async_copy(matrix_ref.at[pl.ds(0, PANEL), place], top_in.at[i], own_sem.at[i])
+        return pltpu.make_async_copy(matrix_ref.at[pl.ds(0, PANEL), place], top_in.at[i], own_sem.at[0])
 
     def start_scatter(p):
         @pl.when((row == 0) & (owner_of(p) == 0) & (p < prompt))
@@ -231,30 +232,33 @@
                 scatter(static_slot(i, 1), side, 1).start()
 
     def pair(p):
-        return send(partial.at[:, unit(p, other)], pair_in.at[p], pair_send.at[p], pair_recv.at[p], partner)
+        return send(partial.at[:, unit(p, other)], pair_in.at[p], pair_send.at[0], pair_recv.at[p], partner)
 
     def chain(p, towards, own):
-        slot = 0 if own else 1
+        slot = way(p, own)
         return send(
-            partial.at[:, unit(p, inner if own else other)], chain_in.at[p, slot],
-            chain_send.at[p, slot], chain_recv.at[p, slot], {"row": row + 2 * (2 * towards - 1)},
+            partial.at[:, unit(p, inner if own else other)], chain_in.at[slot],
+            chain_send.at[0], chain_recv.at[slot], {"row": row + 2 * (2 * towards - 1)},
         )
+
+    def way(p, own):
+        return p if own else pairs + turn_of(p)
 
     joins = outer == last - 1
 
     def give(p):
         place = unit(p, inner)
-        return send(hold.at[:, place], hold.at[:, place], give_send.at[p], give_recv.at[p], partner)
+        return send(hold.at[:, place], hold.at[:, place], give_send.at[0], give_recv.at[p], partner)
 
     def given(p):
         place = unit(p, other)
-        return send(hold.at[:, place], hold.at[:, place], give_send.at[p], give_recv.at[p], partner)
+        return send(hold.at[:, place], hold.at[:, place], give_send.at[0], give_recv.at[p], partner)
 
     def onward(p, owner, own):
         place = unit(p, inner if own else other)
-        slot = 0 if own else 1
+        slot = way(p, own)
         return send(
-            hold.at[:, place], hold.at[:, place], pass_send.at[p, slot], pass_recv.at[p, slot],
+            hold.at[:, place], hold.at[:, place], pass_send.at[0], pass_recv.at[slot],
             {"row": row + 2 * (1 - 2 * owner)},
         )
 
@@ -338,17 +342,17 @@
     def _():
         def part(d):
             q = lax.rem(row + d, n_row)
-            return send(parts.at[q], arrived.at[d - 1], part_send.at[d - 1], part_recv.at[d - 1], {"row": q})
+            return send(parts.at[q], arrived.at[d - 1], part_send.at[0], part_recv.at[0], {"row": q})
 
         def whole_copy(e):
-            return send(whole.at[row], whole.at[row], whole_send.at[e], whole_recv.at[row], {"row": end_rows[e]})
+            return send(whole.at[row], whole.at[row], whole_send.at[0], whole_recv.at[0], {"row": end_rows[e]})
 
         def top_copy(e):
-            return send(panel.at[pl.ds(0, PANEL)], top, top_send.at[e], top_recv.at[0], {"row": end_rows[e]})
+            return send(panel.at[pl.ds(0, PANEL)], top, top_send.at[0], top_recv.at[0], {"row": end_rows[e]})
 
         def share(c, slot):
             ref = (top, whole)[slot]
-            return send(ref, ref, share_send.at[c - 1, slot], share_recv.at[slot], {"col": c})
+            return send(ref, ref, share_send.at[0], share_recv.at[slot], {"col": c})
 
         for d in range(1, n_row):
             part(d).start()
@@ -368,9 +372,9 @@
             load(j).wait()
             multiply(j)
 
+        send(arrived, arrived, part_send.at[0], part_recv.at[0], {"row": 0}).wait_recv()
         total = parts[row]
         for d in range(1, n_row):
-            part(d).wait_recv()
             total = total + arrived[d - 1]
         whole[row] = total
         for e in range(4):
@@ -402,29 +406,10 @@
 
         @pl.when(is_end)
         def _():
-            for q in range(n_row):
-                @pl.when(row != q)
-                def _():
-                    send(whole.at[q], whole.at[q], whole_send.at[0], whole_recv.at[q], {"row": q}).wait_recv()
+            most = whole.at[pl.ds(0, n_row - 1)]
+            send(most, most, whole_send.at[0], whole_recv.at[0], {"row": 0}).wait_recv()
             for c in range(1, n_col):
                 share(c, 1).start()
-            for c in range(1, n_col):
-                share(c, 0).wait_send()
-                share(c, 1).wait_send()
-
-        for d in range(1, n_row):
-            part(d).wait_send()
-        for slot, c in enumerate(heads):
-            panel_copy(c, slot).wait_send()
-        for e in range(4):
-            @pl.when(row != end_rows[e])
-            def _():
-                whole_copy(e).wait_send()
-
-        @pl.when(row == 0)
-        def _():
-            for e in range(1, 4):
-                top_copy(e).wait_send()
 
     @pl.when(col != 0)
     def _():
@@ -455,8 +440,8 @@
 
         @pl.when(is_end)
         def _():
-            send(top, top, share_send.at[0, 0], share_recv.at[0], root).wait_recv()
-            send(whole, whole, share_send.at[0, 1], share_recv.at[1], root).wait_recv()
+            send(top, top, share_send.at[0], share_recv.at[0], root).wait_recv()
+            send(whole, whole, share_send.at[0], share_recv.at[1], root).wait_recv()
 
         @pl.when(relay)
         def _():
@@ -479,14 +464,14 @@
         p = static_slot(i, 0)
         pair(p).wait_recv()
         chain(p, 0, True).wait_recv()
-        add(p, inner, pair_in.at[p], chain_in.at[p, 0])
+        add(p, inner, pair_in.at[p], chain_in.at[p])
         chain(p, 0, True).start()
 
     def relay_up(i):
         p = static_slot(i, 1)
         for own in (False, True):
             chain(p, 1, own).wait_recv()
-            add(p, inner if own else other, chain_in.at[p, 0 if own else 1])
+            add(p, inner if own else other, chain_in.at[way(p, own)])
 
             @pl.when(jnp.logical_not(joins))
             def _():
@@ -558,21 +543,19 @@
         def at_row_zero():
             if held:
                 top_in[i] = block[:PANEL, place]
-            else:
-                keep(i).wait()
 
         def elsewhere():
             if held:
                 top_in[i] = jnp.zeros((PANEL, LANES), jnp.float32)
             else:
-                send(top_in.at[i], top_in.at[i], scatter_send.at[0, 0], scatter_recv.at[i], {"row": 0}).wait_recv()
+                send(top_in.at[i], top_in.at[i], scatter_send.at[0], scatter_recv.at[i], {"row": 0}).wait_recv()
 
         if owner == 0:
             pl.when(row == 0)(at_row_zero)
             pl.when(row != 0)(elsewhere)
         else:
             elsewhere()
-        total = partial[:, place] + pair_in[p] + chain_in[p, 0]
+        total = partial[:, place] + pair_in[p] + chain_in[p]
         hold[:, place] = dot_exact(inverse_ref[...], jnp.concatenate([total, top_in[i]], axis=0), ((1,), (0,)))
         onward(p, owner, True).start()
         give(p).start()
@@ -592,53 +575,59 @@
 
     turns = sorted((static_slot(i, owner), owner, i) for owner in range(2) for i in range(counts[owner]))
 
-    def settle_sums(role):
-        for p, owner, _ in turns:
-            if owner == 0:
-                pair(p).wait_send()
-                if role != 0:
-                    chain(p, 0, True).wait_send()
-            elif role == 0:
-                chain(p, 1, True).wait_send()
-                chain(p, 1, False).wait_send()
-            elif role == 3:
-                pair(p).wait_send()
-            else:
-                chain(p, 1, True).wait_send()
-
-                @pl.when(joins)
-                def _():
-                    pair(p).wait_send()
-
-                @pl.when(jnp.logical_not(joins))
-                def _():
-                    chain(p, 1, False).wait_send()
+    def drain(sem, units):
+        ref = partial.at[:, pl.ds(0, units * LANES)]
+        send(ref, ref, sem.at[0], pair_recv.at[0], partner).wait_send()
+
+    downs, ups = counts
+    prompt_downs = sum(1 for p, owner, _ in turns if owner == 0 and p < prompt)
+    prompt_ups = sum(1 for p, owner, _ in turns if owner == 1 and p < prompt)
+
+    def settle(role):
+        for p, owner, i in turns:
+            if not is_direct(i, owner):
+                given(p).wait_recv()
+        drain(give_send, downs + (ups if role == 3 else 0))
+        drain(pass_send, (downs, downs + 2 * ups, downs + 2 * ups, 2 * ups)[role])
+        if role == 2:
+            @pl.when(joins)
+            def _():
+                drain(pair_send, downs + ups)
+                drain(chain_send, downs + ups)
+
+            @pl.when(jnp.logical_not(joins))
+            def _():
+                drain(pair_send, downs)
+                drain(chain_send, downs + 2 * ups)
+        else:
+            drain(pair_send, downs + (ups if role == 3 else 0))
+            drain(chain_send, (2 * ups, downs + 2 * ups, 0, downs)[role])
         if role == 0:
             @pl.when(row == 0)
             def _():
-                for p, owner, _ in turns:
-                    if owner == 1 and p < prompt:
-                        scatter(p, 0, 1).wait_send()
-                        scatter(p, 1, 1).wait_send()
-                    elif p < prompt:
-                        scatter(p, 1, 0).wait_send()
-
-    def settle_back(role):
-        for owner in range(2):
-            for i in range(counts[owner]):
-                p = static_slot(i, owner)
-                owned = role == (0, 3)[owner]
-                stops = role == (3, 0)[owner]
-                if owned or not is_direct(i, owner):
-                    give(p).wait_send()
-                if not is_direct(i, owner):
-                    given(p).wait_recv()
-                if not stops:
-                    onward(p, owner, True).wait_send()
-                    if is_direct(i, owner):
-                        onward(p, owner, False).wait_send()
+                drain(scatter_send, prompt_downs + 2 * prompt_ups)
+
+        @pl.when(col == 0)
+        def _():
+            for slot, c in enumerate(heads):
+                panel_copy(c, slot).wait_send()
+            send(arrived, arrived, part_send.at[0], part_recv.at[0], {"row": 0}).wait_send()
+            sent = whole.at[pl.ds(0, 3 if role in (0, 3) else 4)]
+            send(sent, sent, whole_send.at[0], whole_recv.at[0], {"row": 0}).wait_send()
+            if role in (0, 3):
+                drain(share_send, 2 * (n_col - 1))
+            if role == 0:
+                @pl.when(row == 0)
+                def _():
+                    drain(top_send, 3)
 
     def follow(role):
+        if role == 0:
+            @pl.when(row == 0)
+            def _():
+                kept = top_in.at[pl.ds(0, prompt_downs)]
+                pltpu.make_async_copy(kept, kept, own_sem.at[0]).wait()
+
         for event in plan(role, counts, prompt):
             kind, owner, i = event
             if kind == "solve":
@@ -653,11 +642,9 @@
                 relay_up(i)
             elif kind == "join":
                 join_up(i)
-            elif kind == "sums":
-                settle_sums(role)
             else:
                 accept(i, owner, kind == "own", role == (3, 0)[owner])
-        settle_back(role)
+        settle(role)
 
     pl.when(first)(lambda: follow(0))
     pl.when(jnp.logical_not(is_end) & (near == 0))(lambda: follow(1))
@@ -712,7 +699,7 @@
     piece = PANEL // n_row
     blocks = width // (4 * LANES)
     pairs = 2 * blocks
-    most = owned_counts(pairs)[0]
+    most, ups = owned_counts(pairs)
     dma = pltpu.SemaphoreType.DMA
     f32, bf16 = jnp.float32, jnp.bfloat16
     hold, shifted = pl.pallas_call(
@@ -727,7 +714,7 @@
             pltpu.VMEM((height, width), f32),
             pltpu.VMEM((PANEL, width), f32),
             pltpu.VMEM((pairs, PANEL, LANES), f32),
-            pltpu.VMEM((pairs, 2, PANEL, LANES), f32),
+            pltpu.VMEM((pairs + ups, PANEL, LANES), f32),
             pltpu.VMEM((most, PANEL, LANES), f32),
             pltpu.VMEM((2 * PANEL, height), bf16),
             pltpu.VMEM((height, PANEL), f32),
@@ -739,27 +726,27 @@
             pltpu.VMEM((n_row, piece, PANEL), f32),
             dma((1,)),
             dma((blocks,)),
+            dma((1,)),
+            dma((n_col,)),
+            dma((1,)),
+            dma((1,)),
+            dma((1,)),
+            dma((1,)),
+            dma((1,)),
+            dma((1,)),
+            dma((1,)),
+            dma((1,)),
+            dma((2,)),
+            dma((1,)),
             dma((most,)),
-            dma((n_col,)),
-            dma((1,)),
-            dma((n_row - 1,)),
-            dma((n_row - 1,)),
-            dma((4,)),
-            dma((n_row,)),
-            dma((4,)),
-            dma((1,)),
-            dma((n_col - 1, 2)),
-            dma((2,)),
-            dma((pairs, 2)),
-            dma((most,)),
+            dma((1,)),
             dma((pairs,)),
+            dma((1,)),
+            dma((pairs + ups,)),
+            dma((1,)),
             dma((pairs,)),
-            dma((pairs, 2)),
-            dma((pairs, 2)),
-            dma((pairs,)),
-            dma((pairs,)),
-            dma((pairs, 2)),
-            dma((pairs, 2)),
+            dma((1,)),
+            dma((pairs + ups,)),
         ],
         compiler_params=pltpu.CompilerParams(
             collective_id=0, has_side_effects=True, vmem_limit_bytes=44 * 1024 * 1024

time: 75.1 us -> 71.1 us (0.947)
  Pallas kernels: 74.8 us -> 70.8 us
    pallas_call x1, Pallas kernels: 68 us -> 64 us  [on_device(): pl.pallas_call(functools.partial(step_kernel, n_row, n_col), out_shape=(j...]
where the time goes in v4:
time: 71.1 us; the launch traced here: 71 us
  Pallas kernels  70.8 us (100%)
    pallas_call x1, Pallas kernels, on_device(): pl.pallas_call(functools.partial(step_kernel, n_row, n_col), out_shape=(j...  64 us
    pallas_call x1, Pallas kernels, flush(): pl.pallas_call(flush_kernel, out_shape=jax.ShapeDtypeStruct(block.shape,...  6.77 us

profile of v4, /device:TPU:26, one launch (start us, length us, event | category | flops | bytes accessed | tf_op | source)
XLA Modules:
  0.0 71.0 jit_solution(5082053679108800628)
XLA Ops:
  0.0 0.0 copy-start
  0.0 64.0 %whole_step.1 = (f32[128,4096]{1,0:T(8,128)S(1)}, bf16[768,256]{1,0:T(8,128)(2,1)S(1)}) custom-call(f32[768,4096]{1,0:T(8,128)} %block.1), custom_call_target="tpu_custom_call" | custom-call | tf_op jit(solution)/shard_map/whole_step/pallas_call | solution.py:705
  64.0 0.0 copy-done
  64.1 6.8 %flush.1 = f32[768,4096]{1,0:T(8,128)} custom-call(f32[768,4096]{1,0:T(8,128)S(1)} %copy-done, f32[128,4096]{1,0:T(8,128)S(1)} %get-tuple-element.7.hold, bf16[768,256]{1,0:T(8,128)(2,1)S(1)} %get-tuple-element.8.shifted), custom_call_target="tpu_custom_call" | custom-call | tf_op jit(solution)/shard_map/flush/pallas_call | solution.py:686
Async XLA Ops:
  0.0 64.0 %copy-start = (f32[768,4096]{1,0:T(8,128)S(1)}, f32[768,4096]{1,0:T(8,128)}, u32[]{:S(2)}) copy-start(f32[768,4096]{1,0:T(8,128)} %block.1) | copy-start | bytes 37748740

commit v5 on v4

--- a/solution.py
+++ b/solution.py
@@ -13,9 +13,11 @@
 MESH = pl.DeviceIdType.MESH
 EARLY = 8
 LATE = 7
-UP_SHARE = 4
+UP_SHARE = 5
+UPDATES = 6
 LEAD_PACE = 2.5
 HOP = 4.1
+UPDATE_LAG = 6.0
 
 
 def dot_exact(a, b, contract):
@@ -102,6 +104,12 @@
     return high, (x - high.astype(jnp.float32)).astype(jnp.bfloat16)
 
 
+def product(shifted, values):
+    high, low = split(values)
+    both = jnp.dot(shifted[...], jnp.concatenate([high, high], axis=0), preferred_element_type=jnp.float32)
+    return both + jnp.dot(shifted[:, :PANEL], low, preferred_element_type=jnp.float32)
+
+
 def owned_counts(pairs):
     return pairs - pairs // UP_SHARE, pairs // UP_SHARE
 
@@ -132,6 +140,8 @@
                 put(26.0 + 0.1 * i if owner == 1 else 27.0 + 0.7 * after, "late", owner, i)
         if owner == 0:
             sent = 31.4 + 1.5 * i
+            if i < UPDATES:
+                put(47.0 + i if role == 0 else sent + HOP * role + UPDATE_LAG, "update", 0, i)
             if role == 0:
                 put(27.3 + 0.7 * i, "solve", 0, i)
             else:
@@ -157,8 +167,8 @@
 
 
 def step_kernel(
-    n_row, n_col, matrix_ref, hold, shifted,
-    block, partial, pair_in, chain_in, top_in, stacked, panel, top, factor_ref, inverse_ref,
+    n_row, n_col, matrix_ref, block, hold, shifted,
+    partial, pair_in, chain_in, top_in, stacked, panel, top, factor_ref, inverse_ref,
     parts, arrived, whole,
     fetch_sem, block_sem, own_sem,
     panel_send, panel_recv, part_send, part_recv, whole_send, whole_recv, top_send, top_recv, share_send, share_recv,
@@ -519,6 +529,12 @@
             shifted[:PANEL, :PANEL] = high
             shifted[:PANEL, PANEL:] = low
 
+    def update(i):
+        p = static_slot(i, 0)
+        given(p).wait_recv()
+        place = pl.ds(p * (2 * LANES), 2 * LANES)
+        block[:, place] = block[:, place] - product(shifted, hold[:, place])
+
     def late(i, owner):
         p = static_slot(i, owner)
 
@@ -585,7 +601,7 @@
 
     def settle(role):
         for p, owner, i in turns:
-            if not is_direct(i, owner):
+            if not is_direct(i, owner) and i >= UPDATES:
                 given(p).wait_recv()
         drain(give_send, downs + (ups if role == 3 else 0))
         drain(pass_send, (downs, downs + 2 * ups, downs + 2 * ups, 2 * ups)[role])
@@ -634,6 +650,8 @@
                 solve(i, owner)
             elif kind == "late":
                 late(i, owner)
+            elif kind == "update":
+                update(i)
             elif kind == "pass":
                 pass_other(i, owner)
             elif kind == "down":
@@ -652,43 +670,57 @@
     pl.when(final)(lambda: follow(3))
 
 
-def flush_kernel(block, hold, shifted, out, ring, sem):
+def flush_kernel(n_up, block, hold, shifted, out, ring, sem, done_sem):
     slots = ring.shape[0]
-    pairs = out.shape[1] // (2 * LANES)
+    rest = out.shape[1] // (2 * LANES) - UPDATES
 
     def lanes(p):
-        return pl.ds(pl.multiple_of(p * (2 * LANES), LANES), 2 * LANES)
-
-    def store(p):
-        slot = lax.rem(p, slots)
-        return pltpu.make_async_copy(ring.at[slot], out.at[:, lanes(p)], sem.at[slot])
-
-    @pl.loop(0, pairs)
-    def _(p):
-        @pl.when(p >= slots)
-        def _():
-            store(p - slots).wait()
-
-        high, low = split(hold[:, lanes(p)])
-        both = jnp.dot(shifted[...], jnp.concatenate([high, high], axis=0), preferred_element_type=jnp.float32)
-        rest = jnp.dot(shifted[:, :PANEL], low, preferred_element_type=jnp.float32)
-        ring[lax.rem(p, slots)] = block[:, lanes(p)] - (both + rest)
-        store(p).start()
-
-    @pl.loop(pairs - slots, pairs)
-    def _(p):
-        store(p).wait()
-
-
-def flush(block, hold, shifted):
+        return pl.ds(p * (2 * LANES) if isinstance(p, int) else pl.multiple_of(p * (2 * LANES), LANES), 2 * LANES)
+
+    def place(r):
+        return lanes(jnp.where(r < n_up, 2 * r + 1, r + UPDATES))
+
+    def store(r):
+        slot = lax.rem(r, slots)
+        return pltpu.make_async_copy(ring.at[slot], out.at[:, place(r)], sem.at[slot])
+
+    def done(i):
+        where = lanes(slot_of(i, 0, n_up))
+        return pltpu.make_async_copy(block.at[:, where], out.at[:, where], done_sem.at[i])
+
+    for i in range(UPDATES):
+        done(i).start()
+
+    @pl.loop(0, rest)
+    def _(r):
+        @pl.when(r >= slots)
+        def _():
+            store(r - slots).wait()
+
+        ring[lax.rem(r, slots)] = block[:, place(r)] - product(shifted, hold[:, place(r)])
+        store(r).start()
+
+    for i in range(UPDATES):
+        done(i).wait()
+
+    @pl.loop(rest - slots, rest)
+    def _(r):
+        store(r).wait()
+
+
+def flush(block, hold, shifted, n_up):
     height, width = block.shape
     vmem = pl.BlockSpec(memory_space=pltpu.VMEM)
     return pl.pallas_call(
-        flush_kernel,
+        functools.partial(flush_kernel, n_up),
         out_shape=jax.ShapeDtypeStruct(block.shape, block.dtype),
         in_specs=[vmem] * 3,
         out_specs=pl.BlockSpec(memory_space=pl.ANY),
-        scratch_shapes=[pltpu.VMEM((4, height, 2 * LANES), jnp.float32), pltpu.SemaphoreType.DMA((4,))],
+        scratch_shapes=[
+            pltpu.VMEM((4, height, 2 * LANES), jnp.float32),
+            pltpu.SemaphoreType.DMA((4,)),
+            pltpu.SemaphoreType.DMA((UPDATES,)),
+        ],
         compiler_params=pltpu.CompilerParams(vmem_limit_bytes=16 * 1024 * 1024),
         name="flush",
     )(block, hold, shifted)
@@ -702,16 +734,16 @@
     most, ups = owned_counts(pairs)
     dma = pltpu.SemaphoreType.DMA
     f32, bf16 = jnp.float32, jnp.bfloat16
-    hold, shifted = pl.pallas_call(
+    block, hold, shifted = pl.pallas_call(
         functools.partial(step_kernel, n_row, n_col),
         out_shape=(
+            jax.ShapeDtypeStruct((height, width), f32),
             jax.ShapeDtypeStruct((PANEL, width), f32),
             jax.ShapeDtypeStruct((height, 2 * PANEL), bf16),
         ),
         in_specs=[pl.BlockSpec(memory_space=pltpu.HBM)],
-        out_specs=(pl.BlockSpec(memory_space=pltpu.VMEM),) * 2,
+        out_specs=(pl.BlockSpec(memory_space=pltpu.VMEM),) * 3,
         scratch_shapes=[
-            pltpu.VMEM((height, width), f32),
             pltpu.VMEM((PANEL, width), f32),
             pltpu.VMEM((pairs, PANEL, LANES), f32),
             pltpu.VMEM((pairs + ups, PANEL, LANES), f32),
@@ -749,11 +781,11 @@
             dma((pairs + ups,)),
         ],
         compiler_params=pltpu.CompilerParams(
-            collective_id=0, has_side_effects=True, vmem_limit_bytes=44 * 1024 * 1024
+            collective_id=0, has_side_effects=True, vmem_limit_bytes=36 * 1024 * 1024
         ),
         name="whole_step",
     )(matrix)
-    return flush(matrix, hold, shifted)
+    return flush(block, hold, shifted, owned_counts(pairs)[1])
 
 
 def solution(mesh):

time: 71.1 us -> 69.5 us (0.977)
  Pallas kernels: 70.8 us -> 69.1 us
    pallas_call x1, Pallas kernels: 6.77 us -> 5.6 us  [flush(): pl.pallas_call(functools.partial(flush_kernel, n_up), out_shape=jax.Shape...]
where the time goes in v5:
time: 69.5 us; the launch traced here: 69.3 us
  Pallas kernels  69.1 us (99%)
    pallas_call x1, Pallas kernels, on_device(): pl.pallas_call(functools.partial(step_kernel, n_row, n_col), out_shape=(j...  63.5 us
    pallas_call x1, Pallas kernels, flush(): pl.pallas_call(functools.partial(flush_kernel, n_up), out_shape=jax.Shape...  5.6 us

profile of v5, /device:TPU:26, one launch (start us, length us, event | category | flops | bytes accessed | tf_op | source)
XLA Modules:
  0.0 69.3 jit_solution(1504351545306595321)
XLA Ops:
  0.0 63.5 %whole_step.1 = (f32[768,4096]{1,0:T(8,128)S(1)}, f32[128,4096]{1,0:T(8,128)S(1)}, bf16[768,256]{1,0:T(8,128)(2,1)S(1)}) custom-call(f32[768,4096]{1,0:T(8,128)} %matrix_ref.1), custom_call_target="tpu_custom_call" | custom-call | tf_op jit(solution)/shard_map/whole_step/pallas_call | solution.py:737
  63.5 5.6 %flush.1 = f32[768,4096]{1,0:T(8,128)} custom-call(f32[768,4096]{1,0:T(8,128)S(1)} %get-tuple-element.8.block, f32[128,4096]{1,0:T(8,128)S(1)} %get-tuple-element.9.hold, bf16[768,256]{1,0:T(8,128)(2,1)S(1)} %get-tuple-element.10.shifted), custom_call_target="tpu_custom_call" | custom-call | tf_op jit(solution)/shard_map/flush/pallas_call | solution.py:714

commit v6 on v5

--- a/solution.py
+++ b/solution.py
@@ -15,7 +15,7 @@
 LATE = 7
 UP_SHARE = 5
 UPDATES = 6
-LEAD_PACE = 2.5
+LEAD_PACE = 1.6
 HOP = 4.1
 UPDATE_LAG = 6.0
 
@@ -154,10 +154,10 @@
             near, away, join, solved = 34.0 + 3.5 * after, 37.5 + 3.5 * after, 41.0 + 3.5 * after, 46.0 + 3.0 * after
         if role == 3:
             put(solved, "solve", 1, i)
-            put(solved + 4.5, "pass", 1, i)
+            put(solved + 8.0, "pass", 1, i)
         else:
             put(solved + 1.5 + HOP * (3 - role), "own", 1, i)
-            put(solved + 2.0 + HOP * (4 - role), "other", 1, i)
+            put(solved + 5.0 + HOP * (4 - role), "other", 1, i)
         if role == 1:
             put(near, "up", 1, i)
         if role == 2:

time: 69.5 us -> 68.5 us (0.986)
  Pallas kernels: 69.1 us -> 68.2 us
    pallas_call x1, Pallas kernels: 63.5 us -> 62.6 us  [on_device(): pl.pallas_call(functools.partial(step_kernel, n_row, n_col), out_shape=(j...]
where the time goes in v6:
time: 68.5 us; the launch traced here: 68.4 us
  Pallas kernels  68.2 us (100%)
    pallas_call x1, Pallas kernels, on_device(): pl.pallas_call(functools.partial(step_kernel, n_row, n_col), out_shape=(j...  62.6 us
    pallas_call x1, Pallas kernels, flush(): pl.pallas_call(functools.partial(flush_kernel, n_up), out_shape=jax.Shape...  5.6 us

profile of v6, /device:TPU:26, one launch (start us, length us, event | category | flops | bytes accessed | tf_op | source)
XLA Modules:
  0.0 68.4 jit_solution(17582823908871032873)
XLA Ops:
  0.0 62.6 %whole_step.1 = (f32[768,4096]{1,0:T(8,128)S(1)}, f32[128,4096]{1,0:T(8,128)S(1)}, bf16[768,256]{1,0:T(8,128)(2,1)S(1)}) custom-call(f32[768,4096]{1,0:T(8,128)} %matrix_ref.1), custom_call_target="tpu_custom_call" | custom-call | tf_op jit(solution)/shard_map/whole_step/pallas_call | solution.py:737
  62.6 5.6 %flush.1 = f32[768,4096]{1,0:T(8,128)} custom-call(f32[768,4096]{1,0:T(8,128)S(1)} %get-tuple-element.8.block, f32[128,4096]{1,0:T(8,128)S(1)} %get-tuple-element.9.hold, bf16[768,256]{1,0:T(8,128)(2,1)S(1)} %get-tuple-element.10.shifted), custom_call_target="tpu_custom_call" | custom-call | tf_op jit(solution)/shard_map/flush/pallas_call | solution.py:714

commit v7 on v6

--- a/solution.py
+++ b/solution.py
@@ -17,7 +17,7 @@
 UPDATES = 6
 LEAD_PACE = 1.6
 HOP = 4.1
-UPDATE_LAG = 6.0
+UPDATE_LAG = 8.5
 
 
 def dot_exact(a, b, contract):
@@ -170,7 +170,7 @@
     n_row, n_col, matrix_ref, block, hold, shifted,
     partial, pair_in, chain_in, top_in, stacked, panel, top, factor_ref, inverse_ref,
     parts, arrived, whole,
-    fetch_sem, block_sem, own_sem,
+    go_sem, fetch_sem, block_sem, own_sem,
     panel_send, panel_recv, part_send, part_recv, whole_send, whole_recv, top_send, top_recv, share_send, share_recv,
     scatter_send, scatter_recv, pair_send, pair_recv, chain_send, chain_recv,
     give_send, give_recv, pass_send, pass_recv,
@@ -366,8 +366,8 @@
 
         for d in range(1, n_row):
             part(d).start()
-        for slot, c in enumerate(heads[1:]):
-            panel_copy(c, slot + 1).start()
+        for slot, c in enumerate(heads):
+            panel_copy(c, slot).start()
 
         @pl.when(row == 0)
         def _():
@@ -392,7 +392,7 @@
             def _():
                 whole_copy(e).start()
 
-        panel_copy(heads[0], 0).start()
+        pl.semaphore_signal(go_sem, inc=1, device_id={"col": 1}, device_id_type=MESH)
         for i in range(counts[1]):
             start_up(i)
 
@@ -438,14 +438,28 @@
         def _():
             panel_copy(col + 1, 0).start()
 
+        prepare()
+
         @pl.when(col == 1)
         def _():
+            @pl.loop(0, blocks)
+            def _(j):
+                load(j).wait()
+                multiply(j)
+
+            pl.semaphore_wait(go_sem, 1)
             for i in range(counts[1]):
                 start_up(i)
 
-        prepare()
-        ahead = jnp.where(col == 1, 0, EARLY)
-        multiply_range(0, blocks, ahead)
+            @pl.loop(0, pairs)
+            def _(p):
+                exchange(p)
+                start_scatter(p)
+
+        @pl.when(col != 1)
+        def _():
+            multiply_range(0, blocks, EARLY)
+
         exchange_last()
 
         @pl.when(is_end)
@@ -756,6 +770,7 @@
             pltpu.VMEM((n_row, piece, PANEL), f32),
             pltpu.VMEM((n_row - 1, piece, PANEL), f32),
             pltpu.VMEM((n_row, piece, PANEL), f32),
+            pltpu.SemaphoreType.REGULAR,
             dma((1,)),
             dma((blocks,)),
             dma((1,)),

time: 68.5 us -> 68.3 us (level)
  no operation moved by 1% of the time
where the time goes in v7:
time: 68.3 us; the launch traced here: 68.1 us
  Pallas kernels  67.9 us (99%)
    pallas_call x1, Pallas kernels, on_device(): pl.pallas_call(functools.partial(step_kernel, n_row, n_col), out_shape=(j...  62.3 us
    pallas_call x1, Pallas kernels, flush(): pl.pallas_call(functools.partial(flush_kernel, n_up), out_shape=jax.Shape...  5.59 us

profile of v7, /device:TPU:26, one launch (start us, length us, event | category | flops | bytes accessed | tf_op | source)
XLA Modules:
  0.0 68.1 jit_solution(7572854925889373899)
XLA Ops:
  0.0 62.3 %whole_step.1 = (f32[768,4096]{1,0:T(8,128)S(1)}, f32[128,4096]{1,0:T(8,128)S(1)}, bf16[768,256]{1,0:T(8,128)(2,1)S(1)}) custom-call(f32[768,4096]{1,0:T(8,128)} %matrix_ref.1), custom_call_target="tpu_custom_call" | custom-call | tf_op jit(solution)/shard_map/whole_step/pallas_call | solution.py:751
  62.4 5.6 %flush.1 = f32[768,4096]{1,0:T(8,128)} custom-call(f32[768,4096]{1,0:T(8,128)S(1)} %get-tuple-element.8.block, f32[128,4096]{1,0:T(8,128)S(1)} %get-tuple-element.9.hold, bf16[768,256]{1,0:T(8,128)(2,1)S(1)} %get-tuple-element.10.shifted), custom_call_target="tpu_custom_call" | custom-call | tf_op jit(solution)/shard_map/flush/pallas_call | solution.py:728
